TPU v7x, 256 devices: a whole 4x4x8 slice. The times are simulated.
256 devices in a mesh: lat: 8 (over x, core), lon: 32 (over z, y).
Axes of the slice: x: 4, y: 4, z: 8, core: 2. Of those that a mesh axis runs over, the one named last changes fastest.
Arguments:
- features: bfloat16 [256, 512, 768], P('lat', 'lon'), may hold values from -6 to 6
- cotangent: bfloat16 [256, 512, 768], P('lat', 'lon'), may hold values from -6 to 6
- weight_first: bfloat16 [2, 8, 96, 96], replicated, may hold values from -1 to 1
- weight_second: bfloat16 [2, 8, 96, 96], replicated, may hold values from -1 to 1
Outputs:
- mixed_field: bfloat16 [256, 512, 768], P('lat', 'lon')
- feature_grad: bfloat16 [256, 512, 768], P('lat', 'lon')
- grad_first: float32 [2, 8, 96, 96], replicated
- grad_second: float32 [2, 8, 96, 96], replicated
All inputs are finite; a program needn't handle non-finite values.
Results may differ from a plain program's by a relative error of at most 0.012.
The roundings to bfloat16 on the way count: a program that leaves them out, or rounds other values in their place, can miss the bound.
Values may be sent and summed in bfloat16 or wider, within the bound.
A program may use at most 64 MiB of HBM per device.

v0:
```python
import math

import jax
import jax.numpy as jnp
from jax import lax
from jax.sharding import PartitionSpec as P

NB = 8
BS = 96
KWD = 1


shrink_level = 0.01
gelu_coeff = 0.7978845608028654


def wave_table(first, second, length):
    product = first[:, None] * second[None, :] % length
    angle = 2.0 * math.pi / length * product.astype(jnp.float32)
    return (jnp.cos(angle) / math.sqrt(length), jnp.sin(angle) / math.sqrt(length))


def batch_product(left, weights):
    return jnp.einsum("mbi,bio->mbo", left, weights, preferred_element_type=jnp.float32)


def batch_back(left, weights):
    return jnp.einsum("mbo,bio->mbi", left, weights, preferred_element_type=jnp.float32)


def batch_outer(left, right):
    return jnp.einsum("mbi,mbo->bio", left, right, preferred_element_type=jnp.float32)


def gelu_parts(values):
    squared = values * values
    tangent = jnp.tanh(gelu_coeff * (values + 0.044715 * squared * values))
    result = 0.5 * values * (1.0 + tangent)
    slope = 0.5 * (1.0 + tangent) + 0.5 * values * (1.0 - tangent * tangent) * gelu_coeff * (
        1.0 + 3.0 * 0.044715 * squared
    )
    return (result, slope)


def shrink_parts(values):
    ratio = jnp.tanh(values / shrink_level)
    return (values - shrink_level * ratio, ratio * ratio)


def spectral_block(real_in, imag_in, real_cot, imag_cot, mode_weight, weight_first, weight_second):
    first_re, first_im = (weight_first[0], weight_first[1])
    second_re, second_im = (weight_second[0], weight_second[1])
    pre_real = batch_product(real_in, first_re) - batch_product(imag_in, first_im)
    pre_imag = batch_product(real_in, first_im) + batch_product(imag_in, first_re)
    act_real, slope_real = gelu_parts(pre_real)
    act_imag, slope_imag = gelu_parts(pre_imag)
    hidden_real = act_real.astype(jnp.bfloat16)
    hidden_imag = act_imag.astype(jnp.bfloat16)
    post_real = batch_product(hidden_real, second_re) - batch_product(hidden_imag, second_im)
    post_imag = batch_product(hidden_real, second_im) + batch_product(hidden_imag, second_re)
    shr_real, pass_real = shrink_parts(post_real)
    shr_imag, pass_imag = shrink_parts(post_imag)
    out_real = shr_real.astype(jnp.bfloat16)
    out_imag = shr_imag.astype(jnp.bfloat16)
    grad_post_real = (mode_weight * real_cot.astype(jnp.float32) * pass_real).astype(jnp.bfloat16)
    grad_post_imag = (mode_weight * imag_cot.astype(jnp.float32) * pass_imag).astype(jnp.bfloat16)
    grad_hid_real = batch_back(grad_post_real, second_re) + batch_back(grad_post_imag, second_im)
    grad_hid_imag = batch_back(grad_post_imag, second_re) - batch_back(grad_post_real, second_im)
    grad_pre_real = (grad_hid_real * slope_real).astype(jnp.bfloat16)
    grad_pre_imag = (grad_hid_imag * slope_imag).astype(jnp.bfloat16)
    back_real = (batch_back(grad_pre_real, first_re) + batch_back(grad_pre_imag, first_im)).astype(
        jnp.bfloat16
    )
    back_imag = (batch_back(grad_pre_imag, first_re) - batch_back(grad_pre_real, first_im)).astype(
        jnp.bfloat16
    )
    grad_second = jnp.stack(
        [
            batch_outer(hidden_real, grad_post_real) + batch_outer(hidden_imag, grad_post_imag),
            batch_outer(hidden_real, grad_post_imag) - batch_outer(hidden_imag, grad_post_real),
        ]
    )
    grad_first = jnp.stack(
        [
            batch_outer(real_in, grad_pre_real) + batch_outer(imag_in, grad_pre_imag),
            batch_outer(real_in, grad_pre_imag) - batch_outer(imag_in, grad_pre_real),
        ]
    )
    return (out_real, out_imag, back_real, back_imag, grad_first, grad_second)


def lon_transpose(source, split_dim, concat_dim):
    return lax.all_to_all(source, "lon", split_axis=split_dim, concat_axis=concat_dim, tiled=True)


def shards(features, cotangent, weight_first, weight_second):
    lat_count = lax.axis_size("lat")
    lon_count = lax.axis_size("lon")
    lat_index = lax.axis_index("lat")
    lon_index = lax.axis_index("lon")
    band_rows, band_cols, channels = features.shape
    rows_total = band_rows * lat_count
    cols_total = band_cols * lon_count
    rows_each = band_rows // lon_count
    kept_total = KWD * lat_count * lon_count
    stacked = jnp.stack([features, cotangent])
    full_rows = lon_transpose(stacked, 1, 2)
    lon_cos, lon_sin = wave_table(
        jnp.arange(kept_total, dtype=jnp.int32), jnp.arange(cols_total, dtype=jnp.int32), cols_total
    )
    lon_coeffs = jnp.concatenate([lon_cos, lon_sin]).astype(jnp.bfloat16)
    product = jnp.einsum(
        "aw,rwc->rac",
        lon_coeffs,
        full_rows.reshape(2 * rows_each, cols_total, channels),
        preferred_element_type=jnp.float32,
    )
    spectral_rows = jnp.stack([product[:, :kept_total], -product[:, kept_total:]], axis=1).astype(
        jnp.bfloat16
    )
    spectral_rows = spectral_rows.reshape(2, rows_each, 2, kept_total, channels)
    gathered = lax.all_to_all(
        lax.all_to_all(spectral_rows, "lat", split_axis=3, concat_axis=1, tiled=True),
        "lon",
        split_axis=3,
        concat_axis=1,
        tiled=True,
    )
    position = jnp.arange(rows_total, dtype=jnp.int32)
    row_of = (
        position // rows_each % lat_count * band_rows
        + position // (lat_count * rows_each) * rows_each
        + position % rows_each
    )
    lat_cos, lat_sin = wave_table(jnp.arange(rows_total, dtype=jnp.int32), row_of, rows_total)
    lat_coeffs = jnp.concatenate([lat_cos, lat_sin]).astype(jnp.bfloat16)
    product = jnp.einsum(
        "ah,shrc->sarc",
        lat_coeffs,
        gathered.reshape(2, rows_total, 2, KWD * channels),
        preferred_element_type=jnp.float32,
    )
    upper = product[:, :rows_total]
    lower = product[:, rows_total:]
    spec_real = (upper[:, :, 0] + lower[:, :, 1]).astype(jnp.bfloat16)
    spec_imag = (upper[:, :, 1] - lower[:, :, 0]).astype(jnp.bfloat16)
    modes = rows_total * KWD
    held_kw = (lat_index * lon_count + lon_index) * KWD + jnp.arange(KWD, dtype=jnp.int32)
    mode_weight = jnp.broadcast_to(
        jnp.where(held_kw == 0, 1.0, 2.0).astype(jnp.float32)[None, :], (rows_total, KWD)
    ).reshape(modes, 1, 1)
    results = spectral_block(
        spec_real[0].reshape(modes, NB, BS),
        spec_imag[0].reshape(modes, NB, BS),
        spec_real[1].reshape(modes, NB, BS),
        spec_imag[1].reshape(modes, NB, BS),
        mode_weight,
        weight_first,
        weight_second,
    )
    out_real, out_imag, back_real, back_imag, grad_first, grad_second = results
    spec_out = jnp.stack(
        [jnp.stack([out_real, out_imag]), jnp.stack([back_real, back_imag])]
    ).reshape(2, 2, rows_total, KWD * channels)
    nat_cos, nat_sin = wave_table(
        jnp.arange(rows_total, dtype=jnp.int32), jnp.arange(rows_total, dtype=jnp.int32), rows_total
    )
    nat_coeffs = jnp.concatenate([nat_cos, nat_sin]).astype(jnp.bfloat16)
    product = jnp.einsum("ak,sqkc->saqc", nat_coeffs, spec_out, preferred_element_type=jnp.float32)
    upper = product[:, :rows_total]
    lower = product[:, rows_total:]
    inverse_rows = jnp.stack(
        [upper[:, :, 0] - lower[:, :, 1], lower[:, :, 0] + upper[:, :, 1]], axis=2
    ).astype(jnp.bfloat16)
    inverse_rows = inverse_rows.reshape(2, rows_total, 2, KWD, channels)
    returned = lax.all_to_all(
        lax.all_to_all(inverse_rows, "lat", split_axis=1, concat_axis=3, tiled=True),
        "lon",
        split_axis=1,
        concat_axis=3,
        tiled=True,
    )
    slot_index = jnp.arange(kept_total, dtype=jnp.int32)
    kw_of = (
        slot_index // KWD % lat_count * lon_count + slot_index // (lat_count * KWD)
    ) * KWD + slot_index % KWD
    inv_cos, inv_sin = wave_table(kw_of, jnp.arange(cols_total, dtype=jnp.int32), cols_total)
    plain = jnp.concatenate([inv_cos, -inv_sin]).astype(jnp.bfloat16)
    doubled = jnp.where(kw_of == 0, 1.0, 2.0).astype(jnp.float32)
    scaled = (plain.astype(jnp.float32) * jnp.concatenate([doubled, doubled])[:, None]).astype(
        jnp.bfloat16
    )
    returned_flat = returned.reshape(2, rows_each, 2 * kept_total, channels)
    filtered = jnp.einsum(
        "aw,rac->rwc", scaled, returned_flat[0], preferred_element_type=jnp.float32
    ).astype(jnp.bfloat16)
    backward = jnp.einsum(
        "aw,rac->rwc", plain, returned_flat[1], preferred_element_type=jnp.float32
    ).astype(jnp.bfloat16)
    spatial = lon_transpose(jnp.stack([filtered, backward]), 2, 1)
    mixed_field = (features.astype(jnp.float32) + spatial[0].astype(jnp.float32)).astype(
        jnp.bfloat16
    )
    feature_grad = (cotangent.astype(jnp.float32) + spatial[1].astype(jnp.float32)).astype(
        jnp.bfloat16
    )
    summed = lax.psum((grad_first, grad_second), ("lat", "lon"))
    factor = 1.0 / math.sqrt(rows_total * kept_total)
    return (mixed_field, feature_grad, summed[0] * factor, summed[1] * factor)


def solution(mesh):
    in_specs = (P("lat", "lon", None), P("lat", "lon", None), P(), P())
    out_specs = (P("lat", "lon", None), P("lat", "lon", None), P(), P())
    return jax.shard_map(shards, mesh=mesh, in_specs=in_specs, out_specs=out_specs, check_vma=False)
```

profile of v0, /device:TPU:2, one launch (start us, length us, event | category | flops | bytes accessed | tf_op | source)
XLA Modules:
  0.0 520.0 jit_solution(9959263662346330774)
XLA Ops:
  7.2 2.7 pad_maximum_fusion
  9.9 11.5 %all-to-all-start = ((bf16[2,32,16,768]{3,2,0,1:T(8,128)(2,1)}), bf16[2,32,16,768]{3,2,0,1:T(8,128)(2,1)S(1)}, u32[]{:S(2)}, u32[]{:S(2)}) async-start(bf16[2,32,16,768]{3,2,0,1:T(8,128)(2,1)} %pad_maximum_fusion), calls=%async_computation | async-start | bytes 3145728 | tf_op jit(solution)/shard_map/all_to_all | solution.py:93
  21.3 2.2 multiply_convert_fusion.7
  23.6 36.9 %all-to-all-done = bf16[2,32,16,768]{3,2,0,1:T(8,128)(2,1)S(1)} async-done(((bf16[2,32,16,768]{3,2,0,1:T(8,128)(2,1)}), bf16[2,32,16,768]{3,2,0,1:T(8,128)(2,1)S(1)}, u32[]{:S(2)}, u32[]{:S(2)}) %all-to-all-start) | async-done | bytes 1572896 | tf_op jit(solution)/shard_map/all_to_all | solution.py:93
  60.6 1.0 convolution_bitcast_fusion.2
  61.7 0.2 fusion.40
  62.1 1.9 copy.79
  64.0 25.0 %all_to_all.84 = bf16[2,1,2,256,768]{4,0,2,1,3:T(2,128)(2,1)S(1)} all-to-all(bf16[2,1,2,256,768]{4,0,2,1,3:T(2,128)(2,1)S(1)} %copy.79), channel_id=1, replica_groups=mesh['lat'=8,'lon'=32] {'lat'}, dimensions={3} | all-to-all | bytes 3145728 | tf_op jit(solution)/shard_map/all_to_all | solution.py:123
  89.2 2.0 copy.81
  91.2 5.9 %all-to-all-start.2 = ((bf16[2,8,2,32,768]{4,1,2,0,3:T(8,128)(2,1)}), bf16[2,8,2,32,768]{4,1,2,0,3:T(8,128)(2,1)S(1)}, u32[]{:S(2)}, u32[]{:S(2)}) async-start(bf16[2,8,2,32,768]{4,1,2,0,3:T(8,128)(2,1)} %copy.81), calls=%async_computation.2 | async-start | bytes 3145728 | tf_op jit(solution)/shard_map/all_to_all | solution.py:122
  97.2 1.1 multiply_convert_fusion.9
  98.3 1.1 multiply_convert_fusion.12
  99.5 36.3 %all-to-all-done.2 = bf16[2,8,2,32,768]{4,1,2,0,3:T(8,128)(2,1)S(1)} async-done(((bf16[2,8,2,32,768]{4,1,2,0,3:T(8,128)(2,1)}), bf16[2,8,2,32,768]{4,1,2,0,3:T(8,128)(2,1)S(1)}, u32[]{:S(2)}, u32[]{:S(2)}) %all-to-all-start.2) | async-done | bytes 1572896 | tf_op jit(solution)/shard_map/all_to_all | solution.py:122
  135.7 1.0 convolution_bitcast_fusion.1
  136.8 0.4 fusion.4
  137.2 0.6 copy-done.2
  137.8 0.3 fusion.88
  138.1 0.3 fusion.96
  138.5 0.5 multiply_convert_fusion.4
  138.9 0.5 copy-done.7
  139.4 0.3 fusion.84
  139.7 0.3 fusion.76
  140.2 0.5 multiply_convert_fusion.3
  140.7 0.4 subtract_convert_fusion.1
  141.1 0.2 fusion.79
  141.4 0.4 subtract_convert_fusion
  141.8 0.2 fusion.81
  142.1 0.6 fusion.27
  142.7 0.2 fusion.91
  142.9 0.6 fusion.28
  143.5 0.3 fusion.93
  143.8 0.3 fusion.29
  144.1 0.3 fusion.30
  144.3 1.0 convolution_bitcast_fusion
  145.3 0.2 fusion.41
  145.9 3.1 copy.98
  149.0 25.3 %all_to_all.85 = bf16[2,256,2,1,768]{4,0,3,2,1:T(2,128)(2,1)S(1)} all-to-all(bf16[2,256,2,1,768]{4,0,3,2,1:T(2,128)(2,1)} %copy.98), channel_id=1, replica_groups=mesh['lat'=8,'lon'=32] {'lat'}, dimensions={1} | all-to-all | bytes 3145728 | tf_op jit(solution)/shard_map/all_to_all | solution.py:177
  174.5 2.0 copy.100
  176.6 6.0 %all-to-all-start.4 = ((bf16[2,32,2,8,768]{4,3,2,0,1:T(8,128)(2,1)}), bf16[2,32,2,8,768]{4,3,2,0,1:T(8,128)(2,1)S(1)}, u32[]{:S(2)}, u32[]{:S(2)}) async-start(bf16[2,32,2,8,768]{4,3,2,0,1:T(8,128)(2,1)} %copy.100), calls=%async_computation.4 | async-start | bytes 3145728 | tf_op jit(solution)/shard_map/all_to_all | solution.py:176
  182.6 3.2 multiply_convert_fusion.6
  185.8 35.3 %all-to-all-done.4 = bf16[2,32,2,8,768]{4,3,2,0,1:T(8,128)(2,1)S(1)} async-done(((bf16[2,32,2,8,768]{4,3,2,0,1:T(8,128)(2,1)}), bf16[2,32,2,8,768]{4,3,2,0,1:T(8,128)(2,1)S(1)}, u32[]{:S(2)}, u32[]{:S(2)}) %all-to-all-start.4) | async-done | bytes 1572896 | tf_op jit(solution)/shard_map/all_to_all | solution.py:176
  221.3 0.8 copy-done.11
  222.2 0.6 fusion.18
  222.8 0.7 fusion.17
  223.7 3.0 copy.102
  226.6 5.8 %all-to-all-start.5 = ((bf16[2,1,512,768]{3,0,1,2:T(2,128)(2,1)}), bf16[2,1,512,768]{3,0,1,2:T(2,128)(2,1)S(1)}, u32[]{:S(2)}, u32[]{:S(2)}) async-start(bf16[2,1,512,768]{3,0,1,2:T(2,128)(2,1)} %copy.102), calls=%async_computation.5 | async-start | bytes 3145728 | tf_op jit(solution)/shard_map/all_to_all | solution.py:93
  232.5 1.3 fusion.127
  233.8 1.3 fusion.32
  235.1 0.3 fusion.128
  235.4 0.3 fusion.31
  235.7 0.9 pad_maximum_fusion.5
  236.6 0.2 fusion.125
  236.9 0.3 fusion.34
  237.1 0.2 fusion.126
  237.4 0.3 fusion.33
  237.7 0.9 pad_maximum_fusion.4
  238.6 264.8 %all-reduce.3.cloned.1.call-done = (f32[2,8,96,96]{3,2,1,0:T(8,128)}, f32[2,8,96,96]{3,2,1,0:T(8,128)}) async-done(((f32[2,8,96,96]{3,2,1,0:T(8,128)}, f32[2,8,96,96]{3,2,1,0:T(8,128)}), (f32[2,8,96,96]{3,2,1,0:T(8,128)}, f32[2,8,96,96]{3,2,1,0:T(8,128)})) %all-reduce.3.cloned.1.call-update) | async-done | bytes 1179664 | tf_op jit(solution)/shard_map/psum | solution.py:207
  503.4 2.2 broadcast_multiply_fusion
  505.6 0.9 broadcast_multiply_fusion.1
  506.5 2.2 fusion.123
  508.9 1.0 copy-done.8
  509.9 1.1 fusion.13
  511.1 1.0 copy-done.9
  512.1 1.1 fusion.14
  (43 shorter events, 2.0 us)
Async XLA Ops:
  9.9 50.6 %all-to-all-start = ((bf16[2,32,16,768]{3,2,0,1:T(8,128)(2,1)}), bf16[2,32,16,768]{3,2,0,1:T(8,128)(2,1)S(1)}, u32[]{:S(2)}, u32[]{:S(2)}) async-start(bf16[2,32,16,768]{3,2,0,1:T(8,128)(2,1)} %pad_maximum_fusion), calls=%async_computation | async-start | bytes 3145728 | tf_op jit(solution)/shard_map/all_to_all | solution.py:93
  91.2 44.5 %all-to-all-start.2 = ((bf16[2,8,2,32,768]{4,1,2,0,3:T(8,128)(2,1)}), bf16[2,8,2,32,768]{4,1,2,0,3:T(8,128)(2,1)S(1)}, u32[]{:S(2)}, u32[]{:S(2)}) async-start(bf16[2,8,2,32,768]{4,1,2,0,3:T(8,128)(2,1)} %copy.81), calls=%async_computation.2 | async-start | bytes 3145728 | tf_op jit(solution)/shard_map/all_to_all | solution.py:122
  136.8 1.0 copy-start.2
  138.4 1.0 copy-start.7
  141.1 1.8 copy-start.3
  141.8 0.9 copy-start.5
  143.5 0.8 copy-start
  176.6 44.5 %all-to-all-start.4 = ((bf16[2,32,2,8,768]{4,3,2,0,1:T(8,128)(2,1)}), bf16[2,32,2,8,768]{4,3,2,0,1:T(8,128)(2,1)S(1)}, u32[]{:S(2)}, u32[]{:S(2)}) async-start(bf16[2,32,2,8,768]{4,3,2,0,1:T(8,128)(2,1)} %copy.100), calls=%async_computation.4 | async-start | bytes 3145728 | tf_op jit(solution)/shard_map/all_to_all | solution.py:176
  221.2 1.0 copy-start.11
  221.2 1.0 copy-start.12
  226.6 279.9 %all-to-all-start.5 = ((bf16[2,1,512,768]{3,0,1,2:T(2,128)(2,1)}), bf16[2,1,512,768]{3,0,1,2:T(2,128)(2,1)S(1)}, u32[]{:S(2)}, u32[]{:S(2)}) async-start(bf16[2,1,512,768]{3,0,1,2:T(2,128)(2,1)} %copy.102), calls=%async_computation.5 | async-start | bytes 3145728 | tf_op jit(solution)/shard_map/all_to_all | solution.py:93
  232.4 271.0 %all-reduce.3.cloned.1.call-start = ((), (), s32[]{:S(2)}) async-start(), calls=%async_computation.6 | async-start | bytes 3145728 | tf_op jit(solution)/shard_map/psum | solution.py:207
  232.5 2.6 copy-start.6
  233.8 1.6 copy-start.4
  235.7 1.2 copy-start.1
  503.4 2.2 copy-start.10
  508.8 1.1 copy-start.8
  511.0 1.1 copy-start.9
Sparse Core Ops, SparseCore 0:
  239.4 263.9 all-reduce.2
where the time goes:
time: 521 us; the launch traced here: 520 us
  waiting for transfers between devices  373 us (72%)
  blocking collectives  50.3 us (10%)
  starting transfers between devices  29.2 us (6%)
  local copies, waits for them, and re-layouts  19.4 us (4%)
  other arithmetic  19 us (4%)
  between operations  14.6 us (3%)
  matrix products  14.2 us (3%)
    psum x1, waiting for transfers between devices, shards(): summed = lax.psum((grad_first, grad_second), ('lat', 'lon'))  265 us
    all_to_all x2, waiting for transfers between devices, lon_transpose(): lax.all_to_all(source, 'lon', split_axis=split_dim, concat_axis=concat_di...  36.9 us
    all_to_all x1, waiting for transfers between devices, shards(): lax.all_to_all(lax.all_to_all(spectral_rows, 'lat', split_axis=3, concat_...  36.3 us
    all_to_all x1, waiting for transfers between devices, shards(): lax.all_to_all(lax.all_to_all(inverse_rows, 'lat', split_axis=1, concat_a...  35.3 us
    all_to_all x1, blocking collectives, shards(): lax.all_to_all(inverse_rows, 'lat', split_axis=1, concat_axis=3, tiled=True)  25.3 us
    all_to_all x1, blocking collectives, shards(): lax.all_to_all(spectral_rows, 'lat', split_axis=3, concat_axis=1, tiled=T...  25 us
    all_to_all x2, starting transfers between devices, lon_transpose(): lax.all_to_all(source, 'lon', split_axis=split_dim, concat_axis=concat_di...  17.3 us
  transfers between devices with their start and end apart: 5, of which 4 were waited for; matrix products, arithmetic and copies ran while one was open for 3% of the time, Pallas kernels for 0%

commit v1 on v0

v1 whole, which is shorter than its diff:
```python
import math

import jax
import jax.numpy as jnp
import ml_dtypes
import numpy as np
from jax import lax
from jax.experimental import pallas as pl
from jax.experimental.pallas import tpu as pltpu
from jax.sharding import Mesh
from jax.sharding import PartitionSpec as P

NB = 8
BS = 96
BP = 128
NL, NZ, NY = 8, 8, 4
RB = 8
KB = 8
WB = 16
W = 512
H = 256
KW = 256
CB = RB * BS
NP = 32
SHRINK = 0.01
GELU = 0.7978845608028654
MESH = pl.DeviceIdType.MESH
F32 = jnp.float32
BF16 = jnp.bfloat16


def wave_table(first, second, length):
    product = (first[:, None] * second[None, :]) % length
    angle = np.float32(2.0 * math.pi / length) * product.astype(np.float32)
    root = np.float32(math.sqrt(length))
    return (
        (np.cos(angle) / root).astype(ml_dtypes.bfloat16).astype(np.float32),
        (np.sin(angle) / root).astype(ml_dtypes.bfloat16).astype(np.float32),
    )


def tables():
    lon_cos, lon_sin = wave_table(np.arange(KW), np.arange(W), W)
    lon = np.stack([lon_cos.reshape(NP, KB, W), -lon_sin.reshape(NP, KB, W)], axis=1)
    lon = lon.reshape(2 * KW, W)
    doubled = np.full((NP, 2, KB), 2.0, np.float32)
    doubled[0, :, 0] = 1.0
    plain = lon.T
    scaled = plain * doubled.reshape(1, 2 * KW)
    lat_cos, lat_sin = wave_table(np.arange(H), np.arange(H), H)
    cos = lat_cos.reshape(H, NP, RB)
    sin = lat_sin.reshape(H, NP, RB)
    top = np.stack([cos, sin], axis=2)
    low = np.stack([-sin, cos], axis=2)
    lat = np.concatenate([top, low]).reshape(2 * H, 2 * H)
    return [t.astype(ml_dtypes.bfloat16) for t in (lon, lat, lat.T, scaled, plain)]


def dot(a, b):
    return jnp.dot(a, b, preferred_element_type=F32)


def dot_tb(a, b):
    return lax.dot_general(a, b, (((1,), (1,)), ((), ())), preferred_element_type=F32)


def dot_ta(a, b):
    return lax.dot_general(a, b, (((0,), (0,)), ((), ())), preferred_element_type=F32)


def step_of(index, size):
    half = (index + 1) // 2
    return lax.rem(half + (1 - lax.rem(index, 2)) * (size - 2 * half), size)


def kernel(
    feat, cot, wf, ws, t_lon, t_lat, t_inv, t_scaled, t_plain,
    mixed, fgrad, g_first, g_second,
    buf_a, buf_x, buf_t, buf_b, buf_r, buf_s, buf_o, buf_h, buf_slope, buf_pass,
    buf_d, buf_z, buf_e, buf_u, w1, w2, send_sem, recv_sem,
):
    lat = lax.axis_index("lat")
    zed = lax.axis_index("z")
    why = lax.axis_index("y")
    lon_me = zed * NY + why
    lat_me = lat * NY + why

    barrier = pltpu.get_barrier_semaphore()

    def greet_z(i, carry):
        z = lax.rem(zed + i // NY, NZ)
        y = lax.rem(why + lax.rem(i, NY), NY)
        pl.semaphore_signal(barrier, inc=1, device_id=(lat, z, y), device_id_type=MESH)
        return carry

    def greet_l(i, carry):
        other = lax.rem(lat + i // NY, NL)
        y = lax.rem(why + lax.rem(i, NY), NY)
        pl.semaphore_signal(barrier, inc=1, device_id=(other, zed, y), device_id_type=MESH)
        return carry

    lax.fori_loop(1, NP, greet_z, 0)
    lax.fori_loop(NY, NP, greet_l, 0)

    def exchange(phase, s, src, dst, over_z):
        me = lon_me if over_z else lat_me
        send = send_sem.at[phase, s]
        recv = recv_sem.at[phase, s]

        def one(i, carry):
            step = step_of(i // NY, 8)
            y = lax.rem(why + lax.rem(i, NY), NY)
            if over_z:
                major = lax.rem(zed + step, NZ)
                target = (lat, major, y)
            else:
                major = lax.rem(lat + step, NL)
                target = (major, zed, y)
            pltpu.make_async_remote_copy(
                src_ref=src.at[s, major * NY + y],
                dst_ref=dst.at[s, me],
                send_sem=send,
                recv_sem=recv,
                device_id=target,
                device_id_type=MESH,
            ).start()
            return carry

        lax.fori_loop(1, NP, one, 0)
        pltpu.make_async_copy(src.at[s, me], dst.at[s, me], recv).start()

    def arrived(phase, s, dst):
        pltpu.make_async_copy(dst.at[s], dst.at[s], recv_sem.at[phase, s]).wait()

    def left(phase, s, src):
        part = src.at[s, pl.ds(0, NP - 1)]
        pltpu.make_async_copy(part, part, send_sem.at[phase, s]).wait()

    def pack(s, source):
        def body(y, carry):
            rows = [source[y * RB + r] for r in range(RB)]
            for z in range(NZ):
                pieces = [row[:, z * BS : (z + 1) * BS] for row in rows]
                buf_a[s, z * NY + y] = jnp.concatenate(pieces, axis=1)
            return carry

        lax.fori_loop(0, NY, body, 0)

    def widen(pair):
        zero = jnp.zeros((pair.shape[0], BP - BS), pair.dtype)
        return jnp.concatenate([pair[:, :BS], zero, pair[:, BS:], zero], axis=1)

    def swap_out(s, dst):
        def body(d, carry):
            pieces = []
            for j in range(8):
                low = buf_t[pl.ds(d * 128 + j, 8, stride=8), :]
                high = buf_t[pl.ds(d * 128 + 64 + j, 8, stride=8), :]
                both = jnp.concatenate([low, high], axis=0).astype(BF16)
                pieces.append(both[:, :BS])
            dst[s, d] = jnp.concatenate(pieces, axis=1)
            return carry

        lax.fori_loop(0, NP, body, 0)

    def to_t(out, j):
        view = buf_t.reshape(64, 8, 8, BP)
        view[:, 2 * j] = out[:, :BP].reshape(64, 8, BP)
        view[:, 2 * j + 1] = out[:, BP:].reshape(64, 8, BP)

    def lon_forward(s):
        for j in range(4):
            pair = buf_x[s, :, :, 2 * BS * j : 2 * BS * (j + 1)].reshape(W, 2 * BS)
            to_t(dot(t_lon[...], widen(pair)), j)
        swap_out(s, buf_b)

    def lat_forward(s):
        for j in range(4):
            pair = buf_r[s, :, :, 2 * BS * j : 2 * BS * (j + 1)].reshape(2 * H, 2 * BS)
            out = dot(t_lat[...], widen(pair)).astype(BF16)
            buf_s[s, :, 2 * BP * j : 2 * BP * (j + 1)] = out

    def lat_inverse(s):
        for j in range(4):
            to_t(dot(t_inv[...], buf_o[s, :, 2 * BP * j : 2 * BP * (j + 1)]), j)
        swap_out(s, buf_d)

    def lon_inverse(s):
        table = t_plain if s else t_scaled
        for j in range(3):
            part = buf_z[s, :, :, 2 * BP * j : 2 * BP * (j + 1)].reshape(2 * KW, 2 * BP)
            out = dot(table[...], part).astype(BF16)
            buf_e[s, :, :, 2 * BP * j : 2 * BP * (j + 1)] = out.reshape(NP, WB, 2 * BP)

    def modes(s, k):
        lanes = pl.ds(pl.multiple_of(k * BP, BP), BP)
        return jnp.concatenate([buf_s[s, :H, lanes], buf_s[s, H:, lanes]], axis=1)

    def put_modes(s, k, value):
        lanes = pl.ds(pl.multiple_of(k * BP, BP), BP)
        buf_o[s, :H, lanes] = value[:, :BP]
        buf_o[s, H:, lanes] = value[:, BP:]

    def mlp_forward(k, carry):
        pre = dot(modes(0, k), w1[...])
        squared = pre * pre
        tangent = jnp.tanh(GELU * (pre + 0.044715 * squared * pre))
        hidden = (0.5 * pre * (1.0 + tangent)).astype(BF16)
        buf_h[k] = hidden
        buf_slope[k] = 0.5 * (1.0 + tangent) + 0.5 * pre * (1.0 - tangent * tangent) * GELU * (
            1.0 + 3.0 * 0.044715 * squared
        )
        post = dot(hidden, w2[...])
        ratio = jnp.tanh(post / SHRINK)
        put_modes(0, k, (post - SHRINK * ratio).astype(BF16))
        weight = jnp.where(lat_me * KB + k == 0, 1.0, 2.0).astype(F32)
        buf_pass[k] = weight * (ratio * ratio)
        return carry

    g_first[...] = jnp.zeros_like(g_first)
    g_second[...] = jnp.zeros_like(g_second)

    def mlp_backward(k, carry):
        d_post = (modes(1, k).astype(F32) * buf_pass[k]).astype(BF16)
        d_pre = (dot_tb(d_post, w2[...]) * buf_slope[k]).astype(BF16)
        put_modes(1, k, dot_tb(d_pre, w1[...]).astype(BF16))
        g_second[...] += dot_ta(buf_h[k], d_post)
        g_first[...] += dot_ta(modes(0, k), d_pre)
        return carry

    def unpack(s, source, target):
        def body(y, carry):
            blocks = [buf_u[s, z * NY + y] for z in range(NZ)]
            for r in range(RB):
                pieces = [block[:, r * BS : (r + 1) * BS] for block in blocks]
                row = jnp.concatenate(pieces, axis=1).astype(F32)
                target[y * RB + r] = (source[y * RB + r].astype(F32) + row).astype(BF16)
            return carry

        lax.fori_loop(0, NY, body, 0)

    pack(0, feat)
    pl.semaphore_wait(barrier, 2 * NP - NY - 1)
    exchange(0, 0, buf_a, buf_x, True)
    pack(1, cot)
    exchange(0, 1, buf_a, buf_x, True)

    for source, target in ((wf, w1), (ws, w2)):
        target[...] = jnp.zeros_like(target)
        real = source[0, zed]
        imag = source[1, zed]
        target[0:BS, 0:BS] = real
        target[0:BS, BP : BP + BS] = imag
        target[BP : BP + BS, 0:BS] = -imag
        target[BP : BP + BS, BP : BP + BS] = real

    arrived(0, 0, buf_x)
    lon_forward(0)
    exchange(1, 0, buf_b, buf_r, False)
    arrived(1, 0, buf_r)
    lat_forward(0)
    lax.fori_loop(0, KB, mlp_forward, 0)
    lat_inverse(0)
    exchange(2, 0, buf_d, buf_z, False)
    arrived(0, 1, buf_x)
    lon_forward(1)
    exchange(1, 1, buf_b, buf_r, False)
    arrived(2, 0, buf_z)
    lon_inverse(0)
    exchange(3, 0, buf_e, buf_u, True)
    arrived(1, 1, buf_r)
    lat_forward(1)
    lax.fori_loop(0, KB, mlp_backward, 0)
    lat_inverse(1)
    exchange(2, 1, buf_d, buf_z, False)
    arrived(2, 1, buf_z)
    lon_inverse(1)
    exchange(3, 1, buf_e, buf_u, True)
    arrived(3, 0, buf_u)
    unpack(0, feat, mixed)
    arrived(3, 1, buf_u)
    unpack(1, cot, fgrad)
    for s in range(2):
        left(0, s, buf_a)
        left(1, s, buf_b)
        left(2, s, buf_d)
        left(3, s, buf_e)


def fold(total):
    real = total[:BS, :BS] + total[BP : BP + BS, BP : BP + BS]
    imag = total[:BS, BP : BP + BS] - total[BP : BP + BS, :BS]
    return jnp.stack([real, imag])


def shards(features, cotangent, weight_first, weight_second):
    vmem = pl.BlockSpec(memory_space=pltpu.VMEM)
    chunks = (2, NP, 16, CB)
    grads = jax.ShapeDtypeStruct((2 * BP, 2 * BP), F32)
    rows = jax.ShapeDtypeStruct(features.shape, BF16)
    mixed, fgrad, g_first, g_second = pl.pallas_call(
        kernel,
        out_shape=(rows, rows, grads, grads),
        in_specs=[vmem] * 9,
        out_specs=[vmem] * 4,
        scratch_shapes=[
            pltpu.VMEM(chunks, BF16),
            pltpu.VMEM(chunks, BF16),
            pltpu.VMEM((4096, BP), F32),
            pltpu.VMEM(chunks, BF16),
            pltpu.VMEM(chunks, BF16),
            pltpu.VMEM((2, 2 * H, KB * BP), BF16),
            pltpu.VMEM((2, 2 * H, KB * BP), BF16),
            pltpu.VMEM((KB, 2 * BP, 2 * BP), BF16),
            pltpu.VMEM((KB, 2 * BP, 2 * BP), F32),
            pltpu.VMEM((KB, 2 * BP, 2 * BP), F32),
            pltpu.VMEM(chunks, BF16),
            pltpu.VMEM(chunks, BF16),
            pltpu.VMEM(chunks, BF16),
            pltpu.VMEM(chunks, BF16),
            pltpu.VMEM((2 * BP, 2 * BP), BF16),
            pltpu.VMEM((2 * BP, 2 * BP), BF16),
            pltpu.SemaphoreType.DMA((4, 2)),
            pltpu.SemaphoreType.DMA((4, 2)),
        ],
        compiler_params=pltpu.CompilerParams(
            collective_id=0, has_side_effects=True, vmem_limit_bytes=48 << 20
        ),
    )(features, cotangent, weight_first, weight_second, *[jnp.asarray(t) for t in tables()])
    summed = lax.psum(jnp.stack([fold(g_first), fold(g_second)]), ("lat", "y"))
    gathered = lax.all_gather(summed, "z", axis=2)
    factor = 1.0 / math.sqrt(H * KW)
    return (mixed, fgrad, gathered[0] * factor, gathered[1] * factor)


def solution(mesh):
    split = Mesh(mesh.devices.reshape(NL, NZ, NY), ("lat", "z", "y"))
    spec = P("lat", ("z", "y"), None)
    return jax.shard_map(
        shards,
        mesh=split,
        in_specs=(spec, spec, P(), P()),
        out_specs=(spec, spec, P(), P()),
        check_vma=False,
    )
```

time: 521 us -> 301 us (0.58)
  waiting for transfers between devices: 373 us -> 153 us
  Pallas kernels: 0 us -> 120 us
  blocking collectives: 50.3 us -> 0 us
  starting transfers between devices: 29.2 us -> 0.08 us
  other arithmetic: 19 us -> 2.25 us
  matrix products: 14.2 us -> 0 us
  local copies, waits for them, and re-layouts: 19.4 us -> 10.8 us
    psum x1, waiting for transfers between devices: 265 us -> 112 us  [shards(): summed = lax.psum(jnp.stack([fold(g_first), fold(g_second)]), ('lat', 'y'))]
    pallas_call x0 -> x1, Pallas kernels: none -> 120 us  [shards(): pl.pallas_call(kernel, out_shape=(rows, rows, grads, grads), in_specs=[vm...]
    all_to_all x4 -> x0, waiting for transfers between devices: 108 us -> none  [the longest x2 36.9 us: lon_transpose(): lax.all_to_all(source, 'lon', split_axis=split_dim, concat_axis=concat_di...]
    all_to_all x2 -> x0, blocking collectives: 50.3 us -> none  [the longest x1 25.3 us: shards(): lax.all_to_all(inverse_rows, 'lat', split_axis=1, concat_axis=3, tiled=True)]
    all_gather x0 -> x1, waiting for transfers between devices: none -> 41.1 us  [shards(): gathered = lax.all_gather(summed, 'z', axis=2)]
    all_to_all x4 -> x0, starting transfers between devices: 29.2 us -> none  [the longest x2 17.3 us: lon_transpose(): lax.all_to_all(source, 'lon', split_axis=split_dim, concat_axis=concat_di...]
    dot_general x29 -> x0, matrix products: 14.2 us -> none  [the longest x8 4.13 us: batch_outer(): jnp.einsum('mbi,mbo->bio', left, right, preferred_element_type=jnp.float32)]
    another operation x13 -> x3, other arithmetic: 13.3 us -> 0.05 us  [the longest x1 0.02 us: fold(): return jnp.stack([real, imag])]
  transfers between devices with their start and end apart: 5 -> 2, of which waited for: 4 -> 2; matrix products, arithmetic and copies ran while one was open for 3% -> 0% of each run, Pallas kernels for 0% -> 0%
where the time goes in v1:
time: 301 us; the launch traced here: 300 us
  waiting for transfers between devices  153 us (51%)
  Pallas kernels  120 us (40%)
  between operations  14.1 us (5%)
  local copies, waits for them, and re-layouts  10.8 us (4%)
    pallas_call x1, Pallas kernels, shards(): pl.pallas_call(kernel, out_shape=(rows, rows, grads, grads), in_specs=[vm...  120 us
    psum x1, waiting for transfers between devices, shards(): summed = lax.psum(jnp.stack([fold(g_first), fold(g_second)]), ('lat', 'y'))  112 us
    all_gather x1, waiting for transfers between devices, shards(): gathered = lax.all_gather(summed, 'z', axis=2)  41.1 us
    unnamed x18, local copies, waits for them, and re-layouts  10.8 us
  transfers between devices with their start and end apart: 2, of which 2 were waited for; matrix products, arithmetic and copies ran while one was open for 0% of the time, Pallas kernels for 0%

profile of v1, /device:TPU:2, one launch (start us, length us, event | category | flops | bytes accessed | tf_op | source)
XLA Modules:
  0.0 300.2 jit_solution(4348476601491873930)
XLA Ops:
  7.2 0.0 all-reduce.2.cloned.1.call-start
  7.2 0.0 copy-start
  7.2 1.0 copy-done
  8.3 0.0 copy-start.1
  8.3 1.0 copy-done.1
  9.3 0.0 copy-start.2
  9.3 1.0 copy-done.2
  10.3 0.0 copy-start.3
  10.3 1.0 copy-done.3
  11.4 0.0 copy-start.4
  11.4 1.0 copy-done.4
  12.4 0.0 copy-start.5
  12.4 1.0 copy-done.5
  13.4 0.0 copy-start.6
  13.4 1.0 copy-done.6
  14.4 119.5 %shard_map.120 = (bf16[32,16,768]{2,1,0:T(8,128)(2,1)S(1)}, bf16[32,16,768]{2,1,0:T(8,128)(2,1)S(1)}, f32[256,256]{1,0:T(8,128)S(1)}, f32[256,256]{1,0:T(8,128)S(1)}) custom-call(bf16[32,16,768]{2,1,0:T(8,128)(2,1)} %feat.1, bf16[32,16,768]{2,1,0:T(8,128)(2,1)} %cot.1, bf16[2,8,96,96]{3,2,1,0:T(8,128)(2,1)S(1)} %copy-done.5, ...), custom_call_target="tpu_custom_call" | custom-call | tf_op jit(solution)/shard_map/pallas_call | solution.py:301
  134.0 0.7 maximum_bitcast_fusion
  134.7 0.0 all-reduce.2.cloned.1.call-update
  134.7 0.0 all-gather.2.cloned.1.call-start
  134.8 112.3 %all-reduce.2.cloned.1.call-done = f32[2,2,1,96,96]{4,3,1,0,2:T(8,128)} async-done(((f32[2,2,1,96,96]{4,3,1,0,2:T(8,128)}), f32[2,2,1,96,96]{4,3,1,0,2:T(8,128)}) %all-reduce.2.cloned.1.call-update) | async-done | bytes 147472 | tf_op jit(solution)/shard_map/psum | solution.py:330
  247.1 0.0 all-gather.2.cloned.1.call-update
  247.1 41.1 %all-gather.2.cloned.1.call-done = f32[2,2,8,96,96]{4,3,1,0,2:T(8,128)} async-done(((f32[2,2,1,96,96]{4,3,1,0,2:T(8,128)}), f32[2,2,8,96,96]{4,3,1,0,2:T(8,128)}) %all-gather.2.cloned.1.call-update) | async-done | bytes 1179664 | tf_op jit(solution)/shard_map/all_gather | solution.py:331
  288.2 1.5 fusion
  289.7 0.9 copy.16
  290.6 0.9 copy.15
  291.6 0.9 copy.20
  292.4 0.9 copy.21
  (3 shorter events, 0.0 us)
Async XLA Ops:
  7.2 239.9 %all-reduce.2.cloned.1.call-start = ((), (), s32[]{:S(2)}) async-start(), calls=%async_computation | async-start | bytes 393216 | tf_op jit(solution)/shard_map/psum | solution.py:330
  7.2 1.0 copy-start
  8.3 1.0 copy-start.1
  9.3 1.0 copy-start.2
  10.3 1.0 copy-start.3
  11.4 1.0 copy-start.4
  12.4 1.0 copy-start.5
  13.4 1.0 copy-start.6
  134.7 153.4 %all-gather.2.cloned.1.call-start = ((), (), s32[]{:S(2)}) async-start(), calls=%async_computation.1 | async-start | bytes 1769472 | tf_op jit(solution)/shard_map/all_gather | solution.py:331
Sparse Core Ops, SparseCore 0:
  134.9 112.1 all-reduce.1
  249.0 39.1 all-gather.1

commit v2 on v1

--- a/solution.py
+++ b/solution.py
@@ -22,6 +22,7 @@
 KW = 256
 CB = RB * BS
 NP = 32
+GR = 48
 SHRINK = 0.01
 GELU = 0.7978845608028654
 MESH = pl.DeviceIdType.MESH
@@ -74,16 +75,30 @@
 
 
 def kernel(
-    feat, cot, wf, ws, t_lon, t_lat, t_inv, t_scaled, t_plain,
-    mixed, fgrad, g_first, g_second,
+    feat_hbm, cot_hbm, wf, ws, h_lon, h_lat, h_inv, h_scaled, h_plain,
+    mixed, fgrad, out_first, out_second,
+    feat, cot, t_lon, t_lat, t_inv, t_scaled, t_plain, g_first, g_second,
     buf_a, buf_x, buf_t, buf_b, buf_r, buf_s, buf_o, buf_h, buf_slope, buf_pass,
     buf_d, buf_z, buf_e, buf_u, w1, w2, send_sem, recv_sem,
+    part_g, part_l, part_p, part_y, part_q, part_z, part_c, g_send, g_recv, load_sem,
 ):
     lat = lax.axis_index("lat")
     zed = lax.axis_index("z")
     why = lax.axis_index("y")
     lon_me = zed * NY + why
     lat_me = lat * NY + why
+
+    loads = [
+        pltpu.make_async_copy(source, target, load_sem.at[i])
+        for i, (source, target) in enumerate(
+            [
+                (feat_hbm, feat), (cot_hbm, cot), (h_lon, t_lon), (h_lat, t_lat),
+                (h_inv, t_inv), (h_scaled, t_scaled), (h_plain, t_plain),
+            ]
+        )
+    ]
+    for load in loads:
+        load.start()
 
     barrier = pltpu.get_barrier_semaphore()
 
@@ -239,9 +254,109 @@
 
         lax.fori_loop(0, NY, body, 0)
 
+    def fold():
+        for which, total in ((0, g_first), (1, g_second)):
+            real = total[:BS, :BP] + total[BP : BP + BS, BP:]
+            imag = total[:BS, BP:] - total[BP : BP + BS, :BP]
+            for ri, plane in ((0, real), (1, imag)):
+                part_g[4 * which + 2 * ri] = plane[:GR]
+                part_g[4 * which + 2 * ri + 1] = plane[GR:]
+
+    def gather(stage, count, source_of, dst, target_of):
+        def one(i, carry):
+            source, target = target_of(i)
+            pltpu.make_async_remote_copy(
+                src_ref=source,
+                dst_ref=dst,
+                send_sem=g_send.at[stage],
+                recv_sem=g_recv.at[stage],
+                device_id=target,
+                device_id_type=MESH,
+            ).start()
+            return carry
+
+        lax.fori_loop(1, count, one, 0)
+        if source_of is not None:
+            pltpu.make_async_copy(source_of, dst, g_recv.at[stage]).start()
+
+    def g_arrived(stage, ref):
+        pltpu.make_async_copy(ref, ref, g_recv.at[stage]).wait()
+
+    def g_left(stage, ref):
+        pltpu.make_async_copy(ref, ref, g_send.at[stage]).wait()
+
+    row = lat // 2
+    core = lax.rem(lat, 2)
+
+    def to_lat(i):
+        other = lax.rem(lat + i, NL)
+        return part_g.at[other], (other, zed, why)
+
+    def to_y(i):
+        return part_p, (lat, zed, lax.rem(why + i, NY))
+
+    def to_z(i):
+        return part_q, (lat, lax.rem(zed + i, NZ), why)
+
+    def to_x(i):
+        return part_z, (2 * lax.rem(row + i, NL // 2) + core, zed, why)
+
+    def grads_lat():
+        fold()
+        gather(0, NL, part_g.at[lat], part_l.at[lat], to_lat)
+
+    def grads_y():
+        g_arrived(0, part_l)
+        total = part_l[0]
+        for i in range(1, NL):
+            total = total + part_l[i]
+        part_p[...] = total
+        gather(1, NY, part_p, part_y.at[why], to_y)
+
+    def grads_z():
+        g_arrived(1, part_y)
+        total = part_y[0]
+        for i in range(1, NY):
+            total = total + part_y[i]
+        part_q[...] = total * (1.0 / math.sqrt(H * KW))
+        gather(2, NZ, part_q, part_z.at[zed], to_z)
+
+    def grads_x():
+        g_arrived(2, part_z)
+        gather(3, NL // 2, part_z, part_c.at[core, row], to_x)
+
+    def mate_copy():
+        return pltpu.make_async_remote_copy(
+            src_ref=part_c.at[core],
+            dst_ref=part_c.at[core],
+            send_sem=g_send.at[4],
+            recv_sem=g_recv.at[4],
+            device_id=(2 * row + 1 - core, zed, why),
+            device_id_type=MESH,
+        )
+
+    def grads_core():
+        g_arrived(3, part_c.at[core])
+        mate_copy().start()
+
+    def grads_out():
+        g_arrived(4, part_c.at[0])
+        for piece in range(NL):
+            target = (out_first, out_second)[piece // 4]
+            rows = slice((piece % 2) * GR, (piece % 2 + 1) * GR)
+            for z in range(NZ):
+                target[(piece // 2) % 2, z, rows, :] = part_c[piece % 2, piece // 2, z][:, :BS]
+        g_left(0, part_g.at[pl.ds(0, NL - 1)])
+        g_left(1, part_y.at[pl.ds(0, NY - 1)])
+        g_left(2, part_z.at[pl.ds(0, NZ - 1)])
+        g_left(3, part_c.at[0, pl.ds(0, NL // 2 - 1)])
+        g_left(4, part_c.at[0])
+
+    loads[0].wait()
     pack(0, feat)
     pl.semaphore_wait(barrier, 2 * NP - NY - 1)
     exchange(0, 0, buf_a, buf_x, True)
+    loads[1].wait()
     pack(1, cot)
     exchange(0, 1, buf_a, buf_x, True)
 
@@ -253,6 +368,8 @@
         target[0:BS, BP : BP + BS] = imag
         target[BP : BP + BS, 0:BS] = -imag
         target[BP : BP + BS, BP : BP + BS] = real
+    for load in loads[2:]:
+        load.wait()
 
     arrived(0, 0, buf_x)
     lon_forward(0)
@@ -271,13 +388,19 @@
     arrived(1, 1, buf_r)
     lat_forward(1)
     lax.fori_loop(0, KB, mlp_backward, 0)
+    grads_lat()
     lat_inverse(1)
     exchange(2, 1, buf_d, buf_z, False)
+    grads_y()
+    grads_z()
     arrived(2, 1, buf_z)
     lon_inverse(1)
     exchange(3, 1, buf_e, buf_u, True)
+    grads_x()
     arrived(3, 0, buf_u)
     unpack(0, feat, mixed)
+    grads_core()
+    grads_out()
     arrived(3, 1, buf_u)
     unpack(1, cot, fgrad)
     for s in range(2):
@@ -287,23 +410,26 @@
         left(3, s, buf_e)
 
 
-def fold(total):
-    real = total[:BS, :BS] + total[BP : BP + BS, BP : BP + BS]
-    imag = total[:BS, BP : BP + BS] - total[BP : BP + BS, :BS]
-    return jnp.stack([real, imag])
-
-
 def shards(features, cotangent, weight_first, weight_second):
     vmem = pl.BlockSpec(memory_space=pltpu.VMEM)
+    hbm = pl.BlockSpec(memory_space=pltpu.HBM)
     chunks = (2, NP, 16, CB)
-    grads = jax.ShapeDtypeStruct((2 * BP, 2 * BP), F32)
+    grads = jax.ShapeDtypeStruct((2, NB, BS, BS), F32)
     rows = jax.ShapeDtypeStruct(features.shape, BF16)
-    mixed, fgrad, g_first, g_second = pl.pallas_call(
+    piece = (GR, BP)
+    return pl.pallas_call(
         kernel,
         out_shape=(rows, rows, grads, grads),
-        in_specs=[vmem] * 9,
+        in_specs=[hbm, hbm, vmem, vmem] + [hbm] * 5,
         out_specs=[vmem] * 4,
         scratch_shapes=[
+            pltpu.VMEM(features.shape, BF16),
+            pltpu.VMEM(features.shape, BF16),
+        ]
+        + [pltpu.VMEM((512, 512), BF16)] * 5
+        + [
+            pltpu.VMEM((2 * BP, 2 * BP), F32),
+            pltpu.VMEM((2 * BP, 2 * BP), F32),
             pltpu.VMEM(chunks, BF16),
             pltpu.VMEM(chunks, BF16),
             pltpu.VMEM((4096, BP), F32),
@@ -322,15 +448,21 @@
             pltpu.VMEM((2 * BP, 2 * BP), BF16),
             pltpu.SemaphoreType.DMA((4, 2)),
             pltpu.SemaphoreType.DMA((4, 2)),
+            pltpu.VMEM((NL,) + piece, F32),
+            pltpu.VMEM((NL,) + piece, F32),
+            pltpu.VMEM(piece, F32),
+            pltpu.VMEM((NY,) + piece, F32),
+            pltpu.VMEM(piece, F32),
+            pltpu.VMEM((NZ,) + piece, F32),
+            pltpu.VMEM((2, NL // 2, NZ) + piece, F32),
+            pltpu.SemaphoreType.DMA((5,)),
+            pltpu.SemaphoreType.DMA((5,)),
+            pltpu.SemaphoreType.DMA((7,)),
         ],
         compiler_params=pltpu.CompilerParams(
-            collective_id=0, has_side_effects=True, vmem_limit_bytes=48 << 20
+            collective_id=0, has_side_effects=True, vmem_limit_bytes=58 << 20
         ),
     )(features, cotangent, weight_first, weight_second, *[jnp.asarray(t) for t in tables()])
-    summed = lax.psum(jnp.stack([fold(g_first), fold(g_second)]), ("lat", "y"))
-    gathered = lax.all_gather(summed, "z", axis=2)
-    factor = 1.0 / math.sqrt(H * KW)
-    return (mixed, fgrad, gathered[0] * factor, gathered[1] * factor)
 
 
 def solution(mesh):

time: 301 us -> 134 us (0.45)
  waiting for transfers between devices: 153 us -> 0 us
  between operations: 14.1 us -> 0.65 us
  Pallas kernels: 120 us -> 125 us
  local copies, waits for them, and re-layouts: 10.8 us -> 5.85 us
    psum x1 -> x0, waiting for transfers between devices: 112 us -> none  [shards(): summed = lax.psum(jnp.stack([fold(g_first), fold(g_second)]), ('lat', 'y'))]
    all_gather x1 -> x0, waiting for transfers between devices: 41.1 us -> none  [shards(): gathered = lax.all_gather(summed, 'z', axis=2)]
    pallas_call x1, Pallas kernels: 120 us -> 125 us  [shards(): pl.pallas_call(kernel, out_shape=(rows, rows, grads, grads), in_specs=[hb...]
    unnamed x18 -> x10, local copies, waits for them, and re-layouts: 10.8 us -> 5.85 us
  transfers between devices with their start and end apart: 2 -> 0, of which waited for: 2 -> 0; matrix products, arithmetic and copies ran while one was open for 0% -> 0% of each run, Pallas kernels for 0% -> 0%
where the time goes in v2:
time: 134 us; the launch traced here: 131 us
  Pallas kernels  125 us (93%)
  local copies, waits for them, and re-layouts  5.85 us (4%)
    pallas_call x1, Pallas kernels, shards(): pl.pallas_call(kernel, out_shape=(rows, rows, grads, grads), in_specs=[hb...  125 us
    unnamed x10, local copies, waits for them, and re-layouts  5.85 us

profile of v2, /device:TPU:2, one launch (start us, length us, event | category | flops | bytes accessed | tf_op | source)
XLA Modules:
  0.0 131.2 jit_solution(17780909690925310931)
XLA Ops:
  0.6 124.7 %shard_map.120 = (bf16[32,16,768]{2,1,0:T(8,128)(2,1)}, bf16[32,16,768]{2,1,0:T(8,128)(2,1)}, f32[2,8,96,96]{3,2,1,0:T(8,128)}, f32[2,8,96,96]{3,2,1,0:T(8,128)}) custom-call(bf16[32,16,768]{2,1,0:T(8,128)(2,1)} %feat_hbm.1, bf16[32,16,768]{2,1,0:T(8,128)(2,1)} %cot_hbm.1, bf16[2,8,96,96]{3,2,1,0:T(8,128)(2,1)} %wf.1, bf16[2,8,96,96]{3,2,1,0:T(8,128)(2,1)} %ws.1, ...), custom_call_target="tpu_custom_call" | custom-call | tf_op jit(solution)/shard_map/pallas_call | solution.py:420
  125.3 0.0 copy-start.2
  125.3 2.1 %copy.17 = bf16[32,16,768]{2,1,0:T(8,128)(2,1)} copy(bf16[32,16,768]{2,1,0:T(8,128)(2,1)} %get-tuple-element.8) | data formatting | bytes 1572864
  127.5 0.0 copy-done.2
  127.5 0.0 copy-start.1
  127.5 0.9 copy.18
  128.3 0.5 copy-done.1
  128.9 0.0 copy-start
  128.9 0.9 copy.19
  129.8 0.5 copy-done
  130.3 0.9 copy.20
Async XLA Ops:
  125.3 2.1 %copy-start.2 = (bf16[32,16,768]{2,1,0:T(8,128)(2,1)S(1)}, bf16[32,16,768]{2,1,0:T(8,128)(2,1)}, u32[]{:S(2)}) copy-start(bf16[32,16,768]{2,1,0:T(8,128)(2,1)} %get-tuple-element.9) | copy-start | bytes 2359300
  127.5 1.4 %copy-start.1 = (f32[2,8,96,96]{3,2,1,0:T(8,128)S(1)}, f32[2,8,96,96]{3,2,1,0:T(8,128)}, u32[]{:S(2)}) copy-start(f32[2,8,96,96]{3,2,1,0:T(8,128)} %get-tuple-element.10) | copy-start | bytes 1769476
  128.9 1.4 %copy-start = (f32[2,8,96,96]{3,2,1,0:T(8,128)S(1)}, f32[2,8,96,96]{3,2,1,0:T(8,128)}, u32[]{:S(2)}) copy-start(f32[2,8,96,96]{3,2,1,0:T(8,128)} %get-tuple-element.11) | copy-start | bytes 1769476

commit v3 on v2

--- a/solution.py
+++ b/solution.py
@@ -20,6 +20,8 @@
 W = 512
 H = 256
 KW = 256
+RH = 4
+CH = RH * BS
 CB = RB * BS
 NP = 32
 GR = 48
@@ -49,12 +51,12 @@
     plain = lon.T
     scaled = plain * doubled.reshape(1, 2 * KW)
     lat_cos, lat_sin = wave_table(np.arange(H), np.arange(H), H)
-    cos = lat_cos.reshape(H, NP, RB)
-    sin = lat_sin.reshape(H, NP, RB)
-    top = np.stack([cos, sin], axis=2)
-    low = np.stack([-sin, cos], axis=2)
+    cos = lat_cos.reshape(H, NP, 2, RH).swapaxes(1, 2)
+    sin = lat_sin.reshape(H, NP, 2, RH).swapaxes(1, 2)
+    top = np.stack([cos, sin], axis=3)
+    low = np.stack([-sin, cos], axis=3)
     lat = np.concatenate([top, low]).reshape(2 * H, 2 * H)
-    return [t.astype(ml_dtypes.bfloat16) for t in (lon, lat, lat.T, scaled, plain)]
+    return np.stack([lon, lat, lat.T, scaled, plain]).astype(ml_dtypes.bfloat16)
 
 
 def dot(a, b):
@@ -75,9 +77,9 @@
 
 
 def kernel(
-    feat_hbm, cot_hbm, wf, ws, h_lon, h_lat, h_inv, h_scaled, h_plain,
+    feat_hbm, cot_hbm, wf, ws, h_tables,
     mixed, fgrad, out_first, out_second,
-    feat, cot, t_lon, t_lat, t_inv, t_scaled, t_plain, g_first, g_second,
+    feat, cot, t_lon, t_lat, t_inv, t_scaled, t_plain, buf_w, g_first, g_second,
     buf_a, buf_x, buf_t, buf_b, buf_r, buf_s, buf_o, buf_h, buf_slope, buf_pass,
     buf_d, buf_z, buf_e, buf_u, w1, w2, send_sem, recv_sem,
     part_g, part_l, part_p, part_y, part_q, part_z, part_c, g_send, g_recv, load_sem,
@@ -92,8 +94,8 @@
         pltpu.make_async_copy(source, target, load_sem.at[i])
         for i, (source, target) in enumerate(
             [
-                (feat_hbm, feat), (cot_hbm, cot), (h_lon, t_lon), (h_lat, t_lat),
-                (h_inv, t_inv), (h_scaled, t_scaled), (h_plain, t_plain),
+                (feat_hbm, feat), (cot_hbm, cot), (h_tables.at[0], t_lon), (h_tables.at[1], t_lat),
+                (h_tables.at[2], t_inv), (h_tables.at[3], t_scaled), (h_tables.at[4], t_plain),
             ]
         )
     ]
@@ -117,95 +119,144 @@
     lax.fori_loop(1, NP, greet_z, 0)
     lax.fori_loop(NY, NP, greet_l, 0)
 
-    def exchange(phase, s, src, dst, over_z):
+    row = lat // 2
+    core = lax.rem(lat, 2)
+
+    def send(phase, t, src, dst, over_z, major, y):
         me = lon_me if over_z else lat_me
-        send = send_sem.at[phase, s]
-        recv = recv_sem.at[phase, s]
-
-        def one(i, carry):
-            step = step_of(i // NY, 8)
-            y = lax.rem(why + lax.rem(i, NY), NY)
-            if over_z:
-                major = lax.rem(zed + step, NZ)
-                target = (lat, major, y)
-            else:
-                major = lax.rem(lat + step, NL)
-                target = (major, zed, y)
+        to = major * NY + y
+        target = (lat, major, y) if over_z else (major, zed, y)
+
+        @pl.when(to != me)
+        def _():
             pltpu.make_async_remote_copy(
-                src_ref=src.at[s, major * NY + y],
-                dst_ref=dst.at[s, me],
-                send_sem=send,
-                recv_sem=recv,
+                src_ref=src.at[t, to],
+                dst_ref=dst.at[t, me],
+                send_sem=send_sem.at[phase, t],
+                recv_sem=recv_sem.at[phase, t],
                 device_id=target,
                 device_id_type=MESH,
             ).start()
+
+        @pl.when(to == me)
+        def _():
+            pltpu.make_async_copy(src.at[t, me], dst.at[t, me], recv_sem.at[phase, t]).start()
+
+    def turn(i):
+        return lax.rem(why + i, NY)
+
+    def arrived(phase, t, dst):
+        pltpu.make_async_copy(dst.at[t], dst.at[t], recv_sem.at[phase, t]).wait()
+
+    def left(phase, t, src):
+        part = src.at[t, pl.ds(0, NP - 1)]
+        pltpu.make_async_copy(part, part, send_sem.at[phase, t]).wait()
+
+    def pack(t, source):
+        def body(y, carry):
+            rows = [source[y * RB + (t % 2) * RH + r] for r in range(RH)]
+            for z in range(NZ):
+                pieces = [r[:, z * BS : (z + 1) * BS] for r in rows]
+                buf_a[t, z * NY + y] = jnp.concatenate(pieces, axis=1)
             return carry
 
-        lax.fori_loop(1, NP, one, 0)
-        pltpu.make_async_copy(src.at[s, me], dst.at[s, me], recv).start()
-
-    def arrived(phase, s, dst):
-        pltpu.make_async_copy(dst.at[s], dst.at[s], recv_sem.at[phase, s]).wait()
-
-    def left(phase, s, src):
-        part = src.at[s, pl.ds(0, NP - 1)]
-        pltpu.make_async_copy(part, part, send_sem.at[phase, s]).wait()
-
-    def pack(s, source):
-        def body(y, carry):
-            rows = [source[y * RB + r] for r in range(RB)]
-            for z in range(NZ):
-                pieces = [row[:, z * BS : (z + 1) * BS] for row in rows]
-                buf_a[s, z * NY + y] = jnp.concatenate(pieces, axis=1)
+        lax.fori_loop(0, NY, body, 0)
+
+    def send_rows(t):
+        def body(i, carry):
+            z = lax.rem(zed + step_of(i // NY, NZ), NZ)
+            send(0, t, buf_a, buf_x, True, z, turn(lax.rem(i, NY)))
             return carry
 
-        lax.fori_loop(0, NY, body, 0)
+        lax.fori_loop(0, NP, body, 0)
 
     def widen(pair):
         zero = jnp.zeros((pair.shape[0], BP - BS), pair.dtype)
         return jnp.concatenate([pair[:, :BS], zero, pair[:, BS:], zero], axis=1)
 
-    def swap_out(s, dst):
-        def body(d, carry):
-            pieces = []
-            for j in range(8):
-                low = buf_t[pl.ds(d * 128 + j, 8, stride=8), :]
-                high = buf_t[pl.ds(d * 128 + 64 + j, 8, stride=8), :]
-                both = jnp.concatenate([low, high], axis=0).astype(BF16)
-                pieces.append(both[:, :BS])
-            dst[s, d] = jnp.concatenate(pieces, axis=1)
-            return carry
-
-        lax.fori_loop(0, NP, body, 0)
-
-    def to_t(out, j):
-        view = buf_t.reshape(64, 8, 8, BP)
-        view[:, 2 * j] = out[:, :BP].reshape(64, 8, BP)
-        view[:, 2 * j + 1] = out[:, BP:].reshape(64, 8, BP)
-
-    def lon_forward(s):
-        for j in range(4):
-            pair = buf_x[s, :, :, 2 * BS * j : 2 * BS * (j + 1)].reshape(W, 2 * BS)
-            to_t(dot(t_lon[...], widen(pair)), j)
-        swap_out(s, buf_b)
+    def lon_forward(t):
+        for j in range(2):
+            pair = buf_x[t, :, :, 2 * BS * j : 2 * BS * (j + 1)].reshape(W, 2 * BS)
+            buf_w[:, 2 * BP * j : 2 * BP * (j + 1)] = widen(pair)
+        view = buf_t.at[pl.ds(0, 512)].reshape(8, 2, RH, KB, BP)
+
+        def chunk(m, carry):
+            x = lax.rem(row + step_of(m, NL // 2), NL // 2)
+            coeffs = t_lon[pl.ds(pl.multiple_of(x * 128, 128), 128), :]
+            for j in range(2):
+                out = dot(coeffs, buf_w[:, 2 * BP * j : 2 * BP * (j + 1)])
+                view[:, :, 2 * j] = out[:, :BP].reshape(8, 2, KB, BP)
+                view[:, :, 2 * j + 1] = out[:, BP:].reshape(8, 2, KB, BP)
+
+            def one(i, inner):
+                major = i // NY
+                y = turn(lax.rem(i, NY))
+                base = (major * NY + y) * 64
+                pieces = [
+                    buf_t[pl.ds(base + k, 8, stride=8), :].astype(BF16)[:, :BS] for k in range(KB)
+                ]
+                buf_b[t, 8 * x + major * NY + y] = jnp.concatenate(pieces, axis=1)
+                send(1, t, buf_b, buf_r, False, 2 * x + major, y)
+                return inner
+
+            return lax.fori_loop(0, 8, one, carry)
+
+        lax.fori_loop(0, NL // 2, chunk, 0)
 
     def lat_forward(s):
         for j in range(4):
-            pair = buf_r[s, :, :, 2 * BS * j : 2 * BS * (j + 1)].reshape(2 * H, 2 * BS)
+            lanes = slice(2 * BS * j, 2 * BS * (j + 1))
+            pair = jnp.concatenate(
+                [buf_r[2 * s + h, :, :, lanes].reshape(H, 2 * BS) for h in range(2)], axis=0
+            )
             out = dot(t_lat[...], widen(pair)).astype(BF16)
             buf_s[s, :, 2 * BP * j : 2 * BP * (j + 1)] = out
 
-    def lat_inverse(s):
-        for j in range(4):
-            to_t(dot(t_inv[...], buf_o[s, :, 2 * BP * j : 2 * BP * (j + 1)]), j)
-        swap_out(s, buf_d)
-
-    def lon_inverse(s):
-        table = t_plain if s else t_scaled
-        for j in range(3):
-            part = buf_z[s, :, :, 2 * BP * j : 2 * BP * (j + 1)].reshape(2 * KW, 2 * BP)
-            out = dot(table[...], part).astype(BF16)
-            buf_e[s, :, :, 2 * BP * j : 2 * BP * (j + 1)] = out.reshape(NP, WB, 2 * BP)
+    def lat_inverse(t):
+        view = buf_t.reshape(16, KB, 8, BP)
+
+        def chunk(m, carry):
+            half = lax.rem(row // 2 + m, 2)
+            start = (t % 2) * H + half * 128
+            coeffs = t_inv[pl.ds(pl.multiple_of(start, 128), 128), :]
+            for j in range(4):
+                out = dot(coeffs, buf_o[t // 2, :, 2 * BP * j : 2 * BP * (j + 1)])
+                view[:, 2 * j] = out[:, :BP].reshape(16, 8, BP)
+                view[:, 2 * j + 1] = out[:, BP:].reshape(16, 8, BP)
+
+            def one(i, inner):
+                major = i // NY
+                y = turn(lax.rem(i, NY))
+                base = (major * NY + y) * 64
+                pieces = []
+                for r in range(RH):
+                    low = buf_t[pl.ds(base + r, 8, stride=8), :]
+                    high = buf_t[pl.ds(base + RH + r, 8, stride=8), :]
+                    pieces.append(jnp.concatenate([low, high], axis=0).astype(BF16)[:, :BS])
+                buf_d[t, 16 * half + major * NY + y] = jnp.concatenate(pieces, axis=1)
+                send(2, t, buf_d, buf_z, False, 4 * half + major, y)
+                return inner
+
+            return lax.fori_loop(0, 16, one, carry)
+
+        lax.fori_loop(0, 2, chunk, 0)
+
+    def lon_inverse(t):
+        table = t_plain if t // 2 else t_scaled
+
+        def chunk(m, carry):
+            pair = lax.rem(zed // 2 + step_of(m, NZ // 2), NZ // 2)
+            coeffs = table[pl.ds(pl.multiple_of(pair * 128, 128), 128), :]
+            out = dot(coeffs, buf_z[t].reshape(2 * KW, CH)).astype(BF16)
+            buf_e[t, pl.ds(pair * 8, 8)] = out.reshape(8, WB, CH)
+
+            def one(i, inner):
+                send(3, t, buf_e, buf_u, True, 2 * pair + i // NY, turn(lax.rem(i, NY)))
+                return inner
+
+            return lax.fori_loop(0, 8, one, carry)
+
+        lax.fori_loop(0, NZ // 2, chunk, 0)
 
     def modes(s, k):
         lanes = pl.ds(pl.multiple_of(k * BP, BP), BP)
@@ -243,13 +294,14 @@
         g_first[...] += dot_ta(modes(0, k), d_pre)
         return carry
 
-    def unpack(s, source, target):
+    def unpack(t, source, target):
         def body(y, carry):
-            blocks = [buf_u[s, z * NY + y] for z in range(NZ)]
-            for r in range(RB):
+            blocks = [buf_u[t, z * NY + y] for z in range(NZ)]
+            for r in range(RH):
                 pieces = [block[:, r * BS : (r + 1) * BS] for block in blocks]
-                row = jnp.concatenate(pieces, axis=1).astype(F32)
-                target[y * RB + r] = (source[y * RB + r].astype(F32) + row).astype(BF16)
+                sums = jnp.concatenate(pieces, axis=1).astype(F32)
+                at = y * RB + (t % 2) * RH + r
+                target[at] = (source[at].astype(F32) + sums).astype(BF16)
             return carry
 
         lax.fori_loop(0, NY, body, 0)
@@ -285,9 +337,6 @@
     def g_left(stage, ref):
         pltpu.make_async_copy(ref, ref, g_send.at[stage]).wait()
 
-    row = lat // 2
-    core = lax.rem(lat, 2)
-
     def to_lat(i):
         other = lax.rem(lat + i, NL)
         return part_g.at[other], (other, zed, why)
@@ -355,10 +404,14 @@
     loads[0].wait()
     pack(0, feat)
     pl.semaphore_wait(barrier, 2 * NP - NY - 1)
-    exchange(0, 0, buf_a, buf_x, True)
+    send_rows(0)
+    pack(1, feat)
+    send_rows(1)
     loads[1].wait()
-    pack(1, cot)
-    exchange(0, 1, buf_a, buf_x, True)
+    pack(2, cot)
+    send_rows(2)
+    pack(3, cot)
+    send_rows(3)
 
     for source, target in ((wf, w1), (ws, w2)):
         target[...] = jnp.zeros_like(target)
@@ -371,70 +424,75 @@
     for load in loads[2:]:
         load.wait()
 
-    arrived(0, 0, buf_x)
-    lon_forward(0)
-    exchange(1, 0, buf_b, buf_r, False)
-    arrived(1, 0, buf_r)
+    for t in (0, 1):
+        arrived(0, t, buf_x)
+        lon_forward(t)
+    for t in (0, 1):
+        arrived(1, t, buf_r)
     lat_forward(0)
     lax.fori_loop(0, KB, mlp_forward, 0)
     lat_inverse(0)
-    exchange(2, 0, buf_d, buf_z, False)
-    arrived(0, 1, buf_x)
-    lon_forward(1)
-    exchange(1, 1, buf_b, buf_r, False)
-    arrived(2, 0, buf_z)
-    lon_inverse(0)
-    exchange(3, 0, buf_e, buf_u, True)
-    arrived(1, 1, buf_r)
+    lat_inverse(1)
+    for t in (2, 3):
+        arrived(0, t, buf_x)
+        lon_forward(t)
+    for t in (0, 1):
+        arrived(2, t, buf_z)
+        lon_inverse(t)
+    for t in (2, 3):
+        arrived(1, t, buf_r)
     lat_forward(1)
     lax.fori_loop(0, KB, mlp_backward, 0)
     grads_lat()
-    lat_inverse(1)
-    exchange(2, 1, buf_d, buf_z, False)
+    lat_inverse(2)
+    lat_inverse(3)
     grads_y()
     grads_z()
-    arrived(2, 1, buf_z)
-    lon_inverse(1)
-    exchange(3, 1, buf_e, buf_u, True)
+    for t in (2, 3):
+        arrived(2, t, buf_z)
+        lon_inverse(t)
     grads_x()
-    arrived(3, 0, buf_u)
-    unpack(0, feat, mixed)
+    for t in (0, 1):
+        arrived(3, t, buf_u)
+        unpack(t, feat, mixed)
     grads_core()
     grads_out()
-    arrived(3, 1, buf_u)
-    unpack(1, cot, fgrad)
-    for s in range(2):
-        left(0, s, buf_a)
-        left(1, s, buf_b)
-        left(2, s, buf_d)
-        left(3, s, buf_e)
+    for t in (2, 3):
+        arrived(3, t, buf_u)
+        unpack(t, cot, fgrad)
+    for t in range(4):
+        left(0, t, buf_a)
+        left(1, t, buf_b)
+        left(2, t, buf_d)
+        left(3, t, buf_e)
 
 
 def shards(features, cotangent, weight_first, weight_second):
     vmem = pl.BlockSpec(memory_space=pltpu.VMEM)
     hbm = pl.BlockSpec(memory_space=pltpu.HBM)
-    chunks = (2, NP, 16, CB)
+    chunks = (4, NP, WB, CH)
+    flat = (4, NP, 8, CB)
     grads = jax.ShapeDtypeStruct((2, NB, BS, BS), F32)
     rows = jax.ShapeDtypeStruct(features.shape, BF16)
     piece = (GR, BP)
     return pl.pallas_call(
         kernel,
         out_shape=(rows, rows, grads, grads),
-        in_specs=[hbm, hbm, vmem, vmem] + [hbm] * 5,
+        in_specs=[hbm, hbm, vmem, vmem, hbm],
         out_specs=[vmem] * 4,
         scratch_shapes=[
             pltpu.VMEM(features.shape, BF16),
             pltpu.VMEM(features.shape, BF16),
         ]
-        + [pltpu.VMEM((512, 512), BF16)] * 5
+        + [pltpu.VMEM((512, 512), BF16)] * 6
         + [
             pltpu.VMEM((2 * BP, 2 * BP), F32),
             pltpu.VMEM((2 * BP, 2 * BP), F32),
             pltpu.VMEM(chunks, BF16),
             pltpu.VMEM(chunks, BF16),
-            pltpu.VMEM((4096, BP), F32),
-            pltpu.VMEM(chunks, BF16),
-            pltpu.VMEM(chunks, BF16),
+            pltpu.VMEM((1024, BP), F32),
+            pltpu.VMEM(flat, BF16),
+            pltpu.VMEM(flat, BF16),
             pltpu.VMEM((2, 2 * H, KB * BP), BF16),
             pltpu.VMEM((2, 2 * H, KB * BP), BF16),
             pltpu.VMEM((KB, 2 * BP, 2 * BP), BF16),
@@ -446,8 +504,8 @@
             pltpu.VMEM(chunks, BF16),
             pltpu.VMEM((2 * BP, 2 * BP), BF16),
             pltpu.VMEM((2 * BP, 2 * BP), BF16),
-            pltpu.SemaphoreType.DMA((4, 2)),
-            pltpu.SemaphoreType.DMA((4, 2)),
+            pltpu.SemaphoreType.DMA((4, 4)),
+            pltpu.SemaphoreType.DMA((4, 4)),
             pltpu.VMEM((NL,) + piece, F32),
             pltpu.VMEM((NL,) + piece, F32),
             pltpu.VMEM(piece, F32),
@@ -462,7 +520,7 @@
         compiler_params=pltpu.CompilerParams(
             collective_id=0, has_side_effects=True, vmem_limit_bytes=58 << 20
         ),
-    )(features, cotangent, weight_first, weight_second, *[jnp.asarray(t) for t in tables()])
+    )(features, cotangent, weight_first, weight_second, jnp.asarray(tables()))
 
 
 def solution(mesh):

time: 134 us -> 125 us (0.933)
  Pallas kernels: 125 us -> 116 us
    pallas_call x1, Pallas kernels: 125 us -> 116 us  [shards(): pl.pallas_call(kernel, out_shape=(rows, rows, grads, grads), in_specs=[hb...]
    unnamed x10 -> x8, local copies, waits for them, and re-layouts: 5.85 us -> 6.01 us
where the time goes in v3:
time: 125 us; the launch traced here: 123 us
  Pallas kernels  116 us (93%)
  local copies, waits for them, and re-layouts  6.01 us (5%)
    pallas_call x1, Pallas kernels, shards(): pl.pallas_call(kernel, out_shape=(rows, rows, grads, grads), in_specs=[hb...  116 us
    unnamed x8, local copies, waits for them, and re-layouts  6.01 us

profile of v3, /device:TPU:2, one launch (start us, length us, event | category | flops | bytes accessed | tf_op | source)
XLA Modules:
  0.0 122.7 jit_solution(441017363460557313)
XLA Ops:
  0.6 116.0 %shard_map.84 = (bf16[32,16,768]{2,1,0:T(8,128)(2,1)}, bf16[32,16,768]{2,1,0:T(8,128)(2,1)}, f32[2,8,96,96]{3,2,1,0:T(8,128)}, f32[2,8,96,96]{3,2,1,0:T(8,128)}) custom-call(bf16[32,16,768]{2,1,0:T(8,128)(2,1)} %feat_hbm.1, bf16[32,16,768]{2,1,0:T(8,128)(2,1)} %cot_hbm.1, bf16[2,8,96,96]{3,2,1,0:T(8,128)(2,1)} %wf.1, bf16[2,8,96,96]{3,2,1,0:T(8,128)(2,1)} %ws.1, ...), custom_call_target="tpu_custom_call" | custom-call | tf_op jit(solution)/shard_map/pallas_call | solution.py:478
  116.6 0.0 copy-start.1
  116.6 0.0 copy-start
  116.6 2.2 %copy.13 = bf16[32,16,768]{2,1,0:T(8,128)(2,1)} copy(bf16[32,16,768]{2,1,0:T(8,128)(2,1)} %get-tuple-element.8) | data formatting | bytes 1572864
  118.8 2.1 %copy.14 = bf16[32,16,768]{2,1,0:T(8,128)(2,1)} copy(bf16[32,16,768]{2,1,0:T(8,128)(2,1)} %get-tuple-element.9) | data formatting | bytes 1572864
  120.9 0.0 copy-done.1
  120.9 0.9 copy.15
  121.8 0.0 copy-done
  121.8 0.9 copy.16
Async XLA Ops:
  116.6 4.3 %copy-start.1 = (f32[2,8,96,96]{3,2,1,0:T(8,128)S(1)}, f32[2,8,96,96]{3,2,1,0:T(8,128)}, u32[]{:S(2)}) copy-start(f32[2,8,96,96]{3,2,1,0:T(8,128)} %get-tuple-element.10) | copy-start | bytes 1769476
  116.6 5.1 %copy-start = (f32[2,8,96,96]{3,2,1,0:T(8,128)S(1)}, f32[2,8,96,96]{3,2,1,0:T(8,128)}, u32[]{:S(2)}) copy-start(f32[2,8,96,96]{3,2,1,0:T(8,128)} %get-tuple-element.11) | copy-start | bytes 1769476

commit v4 on v3

--- a/solution.py
+++ b/solution.py
@@ -27,6 +27,7 @@
 GR = 48
 SHRINK = 0.01
 GELU = 0.7978845608028654
+CUBIC = 0.044715
 MESH = pl.DeviceIdType.MESH
 F32 = jnp.float32
 BF16 = jnp.bfloat16
@@ -78,11 +79,11 @@
 
 def kernel(
     feat_hbm, cot_hbm, wf, ws, h_tables,
-    mixed, fgrad, out_first, out_second,
+    out_rows, out_grads,
     feat, cot, t_lon, t_lat, t_inv, t_scaled, t_plain, buf_w, g_first, g_second,
     buf_a, buf_x, buf_t, buf_b, buf_r, buf_s, buf_o, buf_h, buf_slope, buf_pass,
     buf_d, buf_z, buf_e, buf_u, w1, w2, send_sem, recv_sem,
-    part_g, part_l, part_p, part_y, part_q, part_z, part_c, g_send, g_recv, load_sem,
+    part_g, part_l, part_p, part_y, part_q, part_z, part_c, g_send, g_recv, load_sem, save_sem, ready,
 ):
     lat = lax.axis_index("lat")
     zed = lax.axis_index("z")
@@ -104,20 +105,25 @@
 
     barrier = pltpu.get_barrier_semaphore()
 
-    def greet_z(i, carry):
-        z = lax.rem(zed + i // NY, NZ)
-        y = lax.rem(why + lax.rem(i, NY), NY)
-        pl.semaphore_signal(barrier, inc=1, device_id=(lat, z, y), device_id_type=MESH)
+    def greet(i, carry):
+        z = lax.rem(zed + lax.rem(i, NZ), NZ)
+        other = lax.rem(lat + i, NL)
+        pl.semaphore_signal(barrier, inc=1, device_id=(lat, z, why), device_id_type=MESH)
+        pl.semaphore_signal(barrier, inc=1, device_id=(other, zed, why), device_id_type=MESH)
         return carry
 
-    def greet_l(i, carry):
-        other = lax.rem(lat + i // NY, NL)
-        y = lax.rem(why + lax.rem(i, NY), NY)
-        pl.semaphore_signal(barrier, inc=1, device_id=(other, zed, y), device_id_type=MESH)
-        return carry
-
-    lax.fori_loop(1, NP, greet_z, 0)
-    lax.fori_loop(NY, NP, greet_l, 0)
+    def greet_y(semaphore):
+        for i in range(1, NY):
+            y = lax.rem(why + i, NY)
+            pl.semaphore_signal(semaphore, inc=1, device_id=(lat, zed, y), device_id_type=MESH)
+
+    greet_y(barrier)
+    lax.fori_loop(1, NZ, greet, 0)
+
+    def all_here():
+        pl.semaphore_wait(barrier, NZ + NL + NY - 3)
+        greet_y(ready)
+        pl.semaphore_wait(ready, NY - 1)
 
     row = lat // 2
     core = lax.rem(lat, 2)
@@ -270,14 +276,14 @@
     def mlp_forward(k, carry):
         pre = dot(modes(0, k), w1[...])
         squared = pre * pre
-        tangent = jnp.tanh(GELU * (pre + 0.044715 * squared * pre))
-        hidden = (0.5 * pre * (1.0 + tangent)).astype(BF16)
+        tangent = jnp.tanh(pre * (GELU + (GELU * CUBIC) * squared))
+        gate = 0.5 + 0.5 * tangent
+        active = pre * gate
+        hidden = active.astype(BF16)
         buf_h[k] = hidden
-        buf_slope[k] = 0.5 * (1.0 + tangent) + 0.5 * pre * (1.0 - tangent * tangent) * GELU * (
-            1.0 + 3.0 * 0.044715 * squared
-        )
+        buf_slope[k] = gate + active * (1.0 - tangent) * (GELU + (3.0 * GELU * CUBIC) * squared)
         post = dot(hidden, w2[...])
-        ratio = jnp.tanh(post / SHRINK)
+        ratio = jnp.tanh(post * (1.0 / SHRINK))
         put_modes(0, k, (post - SHRINK * ratio).astype(BF16))
         weight = jnp.where(lat_me * KB + k == 0, 1.0, 2.0).astype(F32)
         buf_pass[k] = weight * (ratio * ratio)
@@ -294,17 +300,9 @@
         g_first[...] += dot_ta(modes(0, k), d_pre)
         return carry
 
-    def unpack(t, source, target):
-        def body(y, carry):
-            blocks = [buf_u[t, z * NY + y] for z in range(NZ)]
-            for r in range(RH):
-                pieces = [block[:, r * BS : (r + 1) * BS] for block in blocks]
-                sums = jnp.concatenate(pieces, axis=1).astype(F32)
-                at = y * RB + (t % 2) * RH + r
-                target[at] = (source[at].astype(F32) + sums).astype(BF16)
-            return carry
-
-        lax.fori_loop(0, NY, body, 0)
+    saves = [
+        pltpu.make_async_copy(buf_u.at[t], out_rows.at[t], save_sem.at[t]) for t in range(4)
+    ] + [pltpu.make_async_copy(part_c, out_grads, save_sem.at[4])]
 
     def fold():
         for which, total in ((0, g_first), (1, g_second)):
@@ -367,7 +365,7 @@
         total = part_y[0]
         for i in range(1, NY):
             total = total + part_y[i]
-        part_q[...] = total * (1.0 / math.sqrt(H * KW))
+        part_q[...] = (total * (1.0 / math.sqrt(H * KW))).astype(BF16)
         gather(2, NZ, part_q, part_z.at[zed], to_z)
 
     def grads_x():
@@ -390,11 +388,7 @@
 
     def grads_out():
         g_arrived(4, part_c.at[0])
-        for piece in range(NL):
-            target = (out_first, out_second)[piece // 4]
-            rows = slice((piece % 2) * GR, (piece % 2 + 1) * GR)
-            for z in range(NZ):
-                target[(piece // 2) % 2, z, rows, :] = part_c[piece % 2, piece // 2, z][:, :BS]
+        saves[4].start()
         g_left(0, part_g.at[pl.ds(0, NL - 1)])
         g_left(1, part_y.at[pl.ds(0, NY - 1)])
         g_left(2, part_z.at[pl.ds(0, NZ - 1)])
@@ -403,7 +397,7 @@
 
     loads[0].wait()
     pack(0, feat)
-    pl.semaphore_wait(barrier, 2 * NP - NY - 1)
+    all_here()
     send_rows(0)
     pack(1, feat)
     send_rows(1)
@@ -427,15 +421,16 @@
     for t in (0, 1):
         arrived(0, t, buf_x)
         lon_forward(t)
+    arrived(0, 2, buf_x)
+    lon_forward(2)
     for t in (0, 1):
         arrived(1, t, buf_r)
     lat_forward(0)
     lax.fori_loop(0, KB, mlp_forward, 0)
     lat_inverse(0)
     lat_inverse(1)
-    for t in (2, 3):
-        arrived(0, t, buf_x)
-        lon_forward(t)
+    arrived(0, 3, buf_x)
+    lon_forward(3)
     for t in (0, 1):
         arrived(2, t, buf_z)
         lon_inverse(t)
@@ -454,17 +449,73 @@
     grads_x()
     for t in (0, 1):
         arrived(3, t, buf_u)
-        unpack(t, feat, mixed)
+        saves[t].start()
     grads_core()
     grads_out()
     for t in (2, 3):
         arrived(3, t, buf_u)
-        unpack(t, cot, fgrad)
+        saves[t].start()
     for t in range(4):
         left(0, t, buf_a)
         left(1, t, buf_b)
         left(2, t, buf_d)
         left(3, t, buf_e)
+    for save in saves:
+        save.wait()
+
+
+def finish_kernel(
+    feat_hbm, cot_hbm, rows_hbm, grads_hbm, mixed_hbm, fgrad_hbm, first_hbm, second_hbm,
+    feat, cot, rows, grads, mixed, fgrad, first, second, load_sem, save_sem, grad_sem,
+):
+    pairs = [(grads_hbm, grads)] + [(rows_hbm.at[t], rows.at[t]) for t in range(4)]
+    pairs[1:1] = [(feat_hbm, feat)]
+    pairs[4:4] = [(cot_hbm, cot)]
+    loads = [
+        pltpu.make_async_copy(source, target, load_sem.at[i])
+        for i, (source, target) in enumerate(pairs)
+    ]
+    for load in loads:
+        load.start()
+
+    loads[0].wait()
+    for piece in range(NL):
+        target = (first, second)[piece // 4]
+        into = slice((piece % 2) * GR, (piece % 2 + 1) * GR)
+        for z in range(NZ):
+            block = grads[piece % 2, piece // 2, z].astype(F32)
+            target[(piece // 2) % 2, z, into, :] = block[:, :BS]
+    grad_saves = [
+        pltpu.make_async_copy(first, first_hbm, grad_sem.at[0]),
+        pltpu.make_async_copy(second, second_hbm, grad_sem.at[1]),
+    ]
+    for save in grad_saves:
+        save.start()
+
+    for s, source, target, out in ((0, feat, mixed, mixed_hbm), (1, cot, fgrad, fgrad_hbm)):
+        for load in loads[1 + 3 * s : 4 + 3 * s]:
+            load.wait()
+
+        def body(y, carry):
+            for h in range(2):
+                blocks = [rows[2 * s + h, z * NY + y] for z in range(NZ)]
+                for r in range(RH):
+                    pieces = [block[:, r * BS : (r + 1) * BS] for block in blocks]
+                    sums = jnp.concatenate(pieces, axis=1).astype(F32)
+                    at = y * RB + h * RH + r
+                    target[at] = (source[at].astype(F32) + sums).astype(BF16)
+            part = pl.ds(y * RB, RB)
+            pltpu.make_async_copy(target.at[part], out.at[part], save_sem.at[s, y]).start()
+            return carry
+
+        lax.fori_loop(0, NY, body, 0)
+
+    for save in grad_saves:
+        save.wait()
+    for s, target, out in ((0, mixed, mixed_hbm), (1, fgrad, fgrad_hbm)):
+        for y in range(NY):
+            part = pl.ds(y * RB, RB)
+            pltpu.make_async_copy(target.at[part], out.at[part], save_sem.at[s, y]).wait()
 
 
 def shards(features, cotangent, weight_first, weight_second):
@@ -475,11 +526,12 @@
     grads = jax.ShapeDtypeStruct((2, NB, BS, BS), F32)
     rows = jax.ShapeDtypeStruct(features.shape, BF16)
     piece = (GR, BP)
-    return pl.pallas_call(
+    gathered = (2, NL // 2, NZ) + piece
+    out_rows, out_grads = pl.pallas_call(
         kernel,
-        out_shape=(rows, rows, grads, grads),
+        out_shape=(jax.ShapeDtypeStruct(chunks, BF16), jax.ShapeDtypeStruct(gathered, BF16)),
         in_specs=[hbm, hbm, vmem, vmem, hbm],
-        out_specs=[vmem] * 4,
+        out_specs=[hbm] * 2,
         scratch_shapes=[
             pltpu.VMEM(features.shape, BF16),
             pltpu.VMEM(features.shape, BF16),
@@ -510,17 +562,39 @@
             pltpu.VMEM((NL,) + piece, F32),
             pltpu.VMEM(piece, F32),
             pltpu.VMEM((NY,) + piece, F32),
-            pltpu.VMEM(piece, F32),
-            pltpu.VMEM((NZ,) + piece, F32),
-            pltpu.VMEM((2, NL // 2, NZ) + piece, F32),
+            pltpu.VMEM(piece, BF16),
+            pltpu.VMEM((NZ,) + piece, BF16),
+            pltpu.VMEM((2, NL // 2, NZ) + piece, BF16),
             pltpu.SemaphoreType.DMA((5,)),
             pltpu.SemaphoreType.DMA((5,)),
             pltpu.SemaphoreType.DMA((7,)),
+            pltpu.SemaphoreType.DMA((5,)),
+            pltpu.SemaphoreType.REGULAR,
         ],
         compiler_params=pltpu.CompilerParams(
             collective_id=0, has_side_effects=True, vmem_limit_bytes=58 << 20
         ),
     )(features, cotangent, weight_first, weight_second, jnp.asarray(tables()))
+    return pl.pallas_call(
+        finish_kernel,
+        out_shape=(rows, rows, grads, grads),
+        in_specs=[hbm] * 4,
+        out_specs=[hbm] * 4,
+        scratch_shapes=[
+            pltpu.VMEM(features.shape, BF16),
+            pltpu.VMEM(features.shape, BF16),
+            pltpu.VMEM(chunks, BF16),
+            pltpu.VMEM(gathered, BF16),
+            pltpu.VMEM(features.shape, BF16),
+            pltpu.VMEM(features.shape, BF16),
+            pltpu.VMEM((2, NB, BS, BS), F32),
+            pltpu.VMEM((2, NB, BS, BS), F32),
+            pltpu.SemaphoreType.DMA((7,)),
+            pltpu.SemaphoreType.DMA((2, NY)),
+            pltpu.SemaphoreType.DMA((2,)),
+        ],
+        compiler_params=pltpu.CompilerParams(vmem_limit_bytes=58 << 20),
+    )(features, cotangent, out_rows, out_grads)
 
 
 def solution(mesh):

time: 125 us -> 116 us (0.928); the launches traced: 123 us -> 116 us
  local copies, waits for them, and re-layouts: 6.01 us -> 0 us
    unnamed x8 -> x0, local copies, waits for them, and re-layouts: 6.01 us -> none
    pallas_call x1 -> x2, Pallas kernels: 116 us -> 115 us  [the longest x1 111 us: shards(): pl.pallas_call(kernel, out_shape=(jax.ShapeDtypeStruct(chunks, BF16), jax...]
where the time goes in v4:
time: 116 us
  Pallas kernels  115 us (99%)
    pallas_call x1, Pallas kernels, shards(): pl.pallas_call(kernel, out_shape=(jax.ShapeDtypeStruct(chunks, BF16), jax...  111 us
    pallas_call x1, Pallas kernels, shards(): pl.pallas_call(finish_kernel, out_shape=(rows, rows, grads, grads), in_sp...  3.6 us

profile of v4, /device:TPU:2, one launch (start us, length us, event | category | flops | bytes accessed | tf_op | source)
XLA Modules:
  0.0 115.6 jit_solution(6889281559841358159)
XLA Ops:
  0.6 111.4 %shard_map.84 = (bf16[4,32,16,384]{3,2,1,0:T(8,128)(2,1)}, bf16[2,4,8,48,128]{4,3,2,1,0:T(8,128)(2,1)}) custom-call(bf16[32,16,768]{2,1,0:T(8,128)(2,1)} %feat_hbm.3, bf16[32,16,768]{2,1,0:T(8,128)(2,1)} %cot_hbm.3, bf16[2,8,96,96]{3,2,1,0:T(8,128)(2,1)} %wf.1, bf16[2,8,96,96]{3,2,1,0:T(8,128)(2,1)} %ws.1, bf16[5,512,512]{2,1,0:T(8,128)(2,1)} %constant.2.clone.h_tables), custom_call_target="tpu_custom_call" | custom-call | tf_op jit(solution)/shard_map/pallas_call | solution.py:530
  112.0 3.6 %shard_map.85 = (bf16[32,16,768]{2,1,0:T(8,128)(2,1)}, bf16[32,16,768]{2,1,0:T(8,128)(2,1)}, f32[2,8,96,96]{3,2,1,0:T(8,128)}, f32[2,8,96,96]{3,2,1,0:T(8,128)}) custom-call(bf16[32,16,768]{2,1,0:T(8,128)(2,1)} %feat_hbm.3, bf16[32,16,768]{2,1,0:T(8,128)(2,1)} %cot_hbm.3, bf16[4,32,16,384]{3,2,1,0:T(8,128)(2,1)} %get-tuple-element.6.rows_hbm, ...), custom_call_target="tpu_custom_call" | custom-call | tf_op jit(solution)/shard_map/pallas_call | solution.py:578

commit v5 on v4

--- a/solution.py
+++ b/solution.py
@@ -81,7 +81,7 @@
     feat_hbm, cot_hbm, wf, ws, h_tables,
     out_rows, out_grads,
     feat, cot, t_lon, t_lat, t_inv, t_scaled, t_plain, buf_w, g_first, g_second,
-    buf_a, buf_x, buf_t, buf_b, buf_r, buf_s, buf_o, buf_h, buf_slope, buf_pass,
+    buf_a, buf_x, buf_t, buf_b, buf_r, buf_s, buf_o, buf_h, buf_slope, buf_pass, buf_dq, buf_dp,
     buf_d, buf_z, buf_e, buf_u, w1, w2, send_sem, recv_sem,
     part_g, part_l, part_p, part_y, part_q, part_z, part_c, g_send, g_recv, load_sem, save_sem, ready,
 ):
@@ -123,18 +123,20 @@
     def all_here():
         pl.semaphore_wait(barrier, NZ + NL + NY - 3)
         greet_y(ready)
+        send_rows(0, (0,))
+        pack(1, feat)
         pl.semaphore_wait(ready, NY - 1)
 
     row = lat // 2
     core = lax.rem(lat, 2)
-
-    def send(phase, t, src, dst, over_z, major, y):
+    odd = lax.rem(zed, 2)
+
+    def send(phase, t, src, dst, over_z, major, y, mine):
         me = lon_me if over_z else lat_me
         to = major * NY + y
         target = (lat, major, y) if over_z else (major, zed, y)
 
-        @pl.when(to != me)
-        def _():
+        def remote():
             pltpu.make_async_remote_copy(
                 src_ref=src.at[t, to],
                 dst_ref=dst.at[t, me],
@@ -144,12 +146,16 @@
                 device_id_type=MESH,
             ).start()
 
-        @pl.when(to == me)
+        if mine is None:
+            remote()
+            return
+        pl.when(jnp.logical_not(mine))(remote)
+
+        @pl.when(mine)
         def _():
             pltpu.make_async_copy(src.at[t, me], dst.at[t, me], recv_sem.at[phase, t]).start()
 
-    def turn(i):
-        return lax.rem(why + i, NY)
+    ys = [lax.rem(why + i, NY) for i in range(NY)]
 
     def arrived(phase, t, dst):
         pltpu.make_async_copy(dst.at[t], dst.at[t], recv_sem.at[phase, t]).wait()
@@ -168,13 +174,14 @@
 
         lax.fori_loop(0, NY, body, 0)
 
-    def send_rows(t):
+    def send_rows(t, turns=(0, 1, 2, 3)):
         def body(i, carry):
-            z = lax.rem(zed + step_of(i // NY, NZ), NZ)
-            send(0, t, buf_a, buf_x, True, z, turn(lax.rem(i, NY)))
+            z = lax.rem(zed + step_of(i, NZ), NZ)
+            for j in turns:
+                send(0, t, buf_a, buf_x, True, z, ys[j], None if j else i == 0)
             return carry
 
-        lax.fori_loop(0, NP, body, 0)
+        lax.fori_loop(0, NZ, body, 0)
 
     def widen(pair):
         zero = jnp.zeros((pair.shape[0], BP - BS), pair.dtype)
@@ -194,18 +201,18 @@
                 view[:, :, 2 * j] = out[:, :BP].reshape(8, 2, KB, BP)
                 view[:, :, 2 * j + 1] = out[:, BP:].reshape(8, 2, KB, BP)
 
-            def one(i, inner):
-                major = i // NY
-                y = turn(lax.rem(i, NY))
-                base = (major * NY + y) * 64
-                pieces = [
-                    buf_t[pl.ds(base + k, 8, stride=8), :].astype(BF16)[:, :BS] for k in range(KB)
-                ]
-                buf_b[t, 8 * x + major * NY + y] = jnp.concatenate(pieces, axis=1)
-                send(1, t, buf_b, buf_r, False, 2 * x + major, y)
-                return inner
-
-            return lax.fori_loop(0, 8, one, carry)
+            for c in range(2):
+                major = core if c == 0 else 1 - core
+                for i, y in enumerate(ys):
+                    base = (major * NY + y) * 64
+                    pieces = [
+                        buf_t[pl.ds(base + k, 8, stride=8), :].astype(BF16)[:, :BS]
+                        for k in range(KB)
+                    ]
+                    buf_b[t, 8 * x + major * NY + y] = jnp.concatenate(pieces, axis=1)
+                    mine = None if c or i else m == 0
+                    send(1, t, buf_b, buf_r, False, 2 * x + major, y, mine)
+            return carry
 
         lax.fori_loop(0, NL // 2, chunk, 0)
 
@@ -230,20 +237,21 @@
                 view[:, 2 * j] = out[:, :BP].reshape(16, 8, BP)
                 view[:, 2 * j + 1] = out[:, BP:].reshape(16, 8, BP)
 
-            def one(i, inner):
-                major = i // NY
-                y = turn(lax.rem(i, NY))
-                base = (major * NY + y) * 64
-                pieces = []
-                for r in range(RH):
-                    low = buf_t[pl.ds(base + r, 8, stride=8), :]
-                    high = buf_t[pl.ds(base + RH + r, 8, stride=8), :]
-                    pieces.append(jnp.concatenate([low, high], axis=0).astype(BF16)[:, :BS])
-                buf_d[t, 16 * half + major * NY + y] = jnp.concatenate(pieces, axis=1)
-                send(2, t, buf_d, buf_z, False, 4 * half + major, y)
+            def one(a, inner):
+                major = lax.rem(lat + a, 4)
+                for i, y in enumerate(ys):
+                    base = (major * NY + y) * 64
+                    pieces = []
+                    for r in range(RH):
+                        low = buf_t[pl.ds(base + r, 8, stride=8), :]
+                        high = buf_t[pl.ds(base + RH + r, 8, stride=8), :]
+                        pieces.append(jnp.concatenate([low, high], axis=0).astype(BF16)[:, :BS])
+                    buf_d[t, 16 * half + major * NY + y] = jnp.concatenate(pieces, axis=1)
+                    mine = None if i else m + a == 0
+                    send(2, t, buf_d, buf_z, False, 4 * half + major, y, mine)
                 return inner
 
-            return lax.fori_loop(0, 16, one, carry)
+            return lax.fori_loop(0, 4, one, carry)
 
         lax.fori_loop(0, 2, chunk, 0)
 
@@ -256,11 +264,12 @@
             out = dot(coeffs, buf_z[t].reshape(2 * KW, CH)).astype(BF16)
             buf_e[t, pl.ds(pair * 8, 8)] = out.reshape(8, WB, CH)
 
-            def one(i, inner):
-                send(3, t, buf_e, buf_u, True, 2 * pair + i // NY, turn(lax.rem(i, NY)))
-                return inner
-
-            return lax.fori_loop(0, 8, one, carry)
+            for c in range(2):
+                major = 2 * pair + (odd if c == 0 else 1 - odd)
+                for i, y in enumerate(ys):
+                    mine = None if c or i else m == 0
+                    send(3, t, buf_e, buf_u, True, major, y, mine)
+            return carry
 
         lax.fori_loop(0, NZ // 2, chunk, 0)
 
@@ -296,8 +305,13 @@
         d_post = (modes(1, k).astype(F32) * buf_pass[k]).astype(BF16)
         d_pre = (dot_tb(d_post, w2[...]) * buf_slope[k]).astype(BF16)
         put_modes(1, k, dot_tb(d_pre, w1[...]).astype(BF16))
-        g_second[...] += dot_ta(buf_h[k], d_post)
-        g_first[...] += dot_ta(modes(0, k), d_pre)
+        buf_dq[k] = d_post
+        buf_dp[k] = d_pre
+        return carry
+
+    def mlp_grads(k, carry):
+        g_second[...] += dot_ta(buf_h[k], buf_dq[k])
+        g_first[...] += dot_ta(modes(0, k), buf_dp[k])
         return carry
 
     saves = [
@@ -398,8 +412,7 @@
     loads[0].wait()
     pack(0, feat)
     all_here()
-    send_rows(0)
-    pack(1, feat)
+    send_rows(0, (1, 2, 3))
     send_rows(1)
     loads[1].wait()
     pack(2, cot)
@@ -426,7 +439,7 @@
     for t in (0, 1):
         arrived(1, t, buf_r)
     lat_forward(0)
-    lax.fori_loop(0, KB, mlp_forward, 0)
+    lax.fori_loop(0, KB, mlp_forward, 0, unroll=2)
     lat_inverse(0)
     lat_inverse(1)
     arrived(0, 3, buf_x)
@@ -437,15 +450,17 @@
     for t in (2, 3):
         arrived(1, t, buf_r)
     lat_forward(1)
-    lax.fori_loop(0, KB, mlp_backward, 0)
-    grads_lat()
+    lax.fori_loop(0, KB, mlp_backward, 0, unroll=2)
     lat_inverse(2)
     lat_inverse(3)
+    lax.fori_loop(0, KB, mlp_grads, 0)
+    grads_lat()
+    arrived(2, 2, buf_z)
+    lon_inverse(2)
     grads_y()
     grads_z()
-    for t in (2, 3):
-        arrived(2, t, buf_z)
-        lon_inverse(t)
+    arrived(2, 3, buf_z)
+    lon_inverse(3)
     grads_x()
     for t in (0, 1):
         arrived(3, t, buf_u)
@@ -550,6 +565,8 @@
             pltpu.VMEM((KB, 2 * BP, 2 * BP), BF16),
             pltpu.VMEM((KB, 2 * BP, 2 * BP), F32),
             pltpu.VMEM((KB, 2 * BP, 2 * BP), F32),
+            pltpu.VMEM((KB, 2 * BP, 2 * BP), BF16),
+            pltpu.VMEM((KB, 2 * BP, 2 * BP), BF16),
             pltpu.VMEM(chunks, BF16),
             pltpu.VMEM(chunks, BF16),
             pltpu.VMEM(chunks, BF16),

time: 116 us -> 110 us (0.948)
  Pallas kernels: 115 us -> 108 us
    pallas_call x1, Pallas kernels: 111 us -> 105 us  [shards(): pl.pallas_call(kernel, out_shape=(jax.ShapeDtypeStruct(chunks, BF16), jax...]
where the time goes in v5:
time: 110 us; the launch traced here: 109 us
  Pallas kernels  108 us (98%)
    pallas_call x1, Pallas kernels, shards(): pl.pallas_call(kernel, out_shape=(jax.ShapeDtypeStruct(chunks, BF16), jax...  105 us
    pallas_call x1, Pallas kernels, shards(): pl.pallas_call(finish_kernel, out_shape=(rows, rows, grads, grads), in_sp...  3.6 us

profile of v5, /device:TPU:2, one launch (start us, length us, event | category | flops | bytes accessed | tf_op | source)
XLA Modules:
  0.0 108.7 jit_solution(12736435863696356751)
XLA Ops:
  0.6 104.5 %shard_map.84 = (bf16[4,32,16,384]{3,2,1,0:T(8,128)(2,1)}, bf16[2,4,8,48,128]{4,3,2,1,0:T(8,128)(2,1)}) custom-call(bf16[32,16,768]{2,1,0:T(8,128)(2,1)} %feat_hbm.3, bf16[32,16,768]{2,1,0:T(8,128)(2,1)} %cot_hbm.3, bf16[2,8,96,96]{3,2,1,0:T(8,128)(2,1)} %wf.1, bf16[2,8,96,96]{3,2,1,0:T(8,128)(2,1)} %ws.1, bf16[5,512,512]{2,1,0:T(8,128)(2,1)} %constant.2.clone.h_tables), custom_call_target="tpu_custom_call" | custom-call | tf_op jit(solution)/shard_map/pallas_call | solution.py:545
  105.1 3.6 %shard_map.85 = (bf16[32,16,768]{2,1,0:T(8,128)(2,1)}, bf16[32,16,768]{2,1,0:T(8,128)(2,1)}, f32[2,8,96,96]{3,2,1,0:T(8,128)}, f32[2,8,96,96]{3,2,1,0:T(8,128)}) custom-call(bf16[32,16,768]{2,1,0:T(8,128)(2,1)} %feat_hbm.3, bf16[32,16,768]{2,1,0:T(8,128)(2,1)} %cot_hbm.3, bf16[4,32,16,384]{3,2,1,0:T(8,128)(2,1)} %get-tuple-element.6.rows_hbm, ...), custom_call_target="tpu_custom_call" | custom-call | tf_op jit(solution)/shard_map/pallas_call | solution.py:595

commit v6 on v5

--- a/solution.py
+++ b/solution.py
@@ -191,30 +191,30 @@
         for j in range(2):
             pair = buf_x[t, :, :, 2 * BS * j : 2 * BS * (j + 1)].reshape(W, 2 * BS)
             buf_w[:, 2 * BP * j : 2 * BP * (j + 1)] = widen(pair)
-        view = buf_t.at[pl.ds(0, 512)].reshape(8, 2, RH, KB, BP)
-
-        def chunk(m, carry):
-            x = lax.rem(row + step_of(m, NL // 2), NL // 2)
-            coeffs = t_lon[pl.ds(pl.multiple_of(x * 128, 128), 128), :]
-            for j in range(2):
-                out = dot(coeffs, buf_w[:, 2 * BP * j : 2 * BP * (j + 1)])
-                view[:, :, 2 * j] = out[:, :BP].reshape(8, 2, KB, BP)
-                view[:, :, 2 * j + 1] = out[:, BP:].reshape(8, 2, KB, BP)
-
-            for c in range(2):
-                major = core if c == 0 else 1 - core
-                for i, y in enumerate(ys):
-                    base = (major * NY + y) * 64
-                    pieces = [
-                        buf_t[pl.ds(base + k, 8, stride=8), :].astype(BF16)[:, :BS]
-                        for k in range(KB)
-                    ]
-                    buf_b[t, 8 * x + major * NY + y] = jnp.concatenate(pieces, axis=1)
-                    mine = None if c or i else m == 0
-                    send(1, t, buf_b, buf_r, False, 2 * x + major, y, mine)
+        def chunk(mm, carry):
+            for p in range(2):
+                m = 2 * mm + p
+                view = buf_t.at[pl.ds(512 * p, 512)].reshape(8, 2, RH, KB, BP)
+                x = lax.rem(row + step_of(m, NL // 2), NL // 2)
+                coeffs = t_lon[pl.ds(pl.multiple_of(x * 128, 128), 128), :]
+                for j in range(2):
+                    out = dot(coeffs, buf_w[:, 2 * BP * j : 2 * BP * (j + 1)])
+                    view[:, :, 2 * j] = out[:, :BP].reshape(8, 2, KB, BP)
+                    view[:, :, 2 * j + 1] = out[:, BP:].reshape(8, 2, KB, BP)
+                for c in range(2):
+                    major = core if c == 0 else 1 - core
+                    for i, y in enumerate(ys):
+                        base = 512 * p + (major * NY + y) * 64
+                        pieces = [
+                            buf_t[pl.ds(base + k, 8, stride=8), :].astype(BF16)[:, :BS]
+                            for k in range(KB)
+                        ]
+                        buf_b[t, 8 * x + major * NY + y] = jnp.concatenate(pieces, axis=1)
+                        mine = None if p or c or i else mm == 0
+                        send(1, t, buf_b, buf_r, False, 2 * x + major, y, mine)
             return carry
 
-        lax.fori_loop(0, NL // 2, chunk, 0)
+        lax.fori_loop(0, NL // 4, chunk, 0)
 
     def lat_forward(s):
         for j in range(4):

time: 110 us -> 111 us (level); the launches traced: 109 us -> 109 us
  no operation moved by 1% of the time
where the time goes in v6:
time: 111 us; the launch traced here: 109 us
  Pallas kernels  108 us (97%)
    pallas_call x1, Pallas kernels, shards(): pl.pallas_call(kernel, out_shape=(jax.ShapeDtypeStruct(chunks, BF16), jax...  104 us
    pallas_call x1, Pallas kernels, shards(): pl.pallas_call(finish_kernel, out_shape=(rows, rows, grads, grads), in_sp...  3.6 us

profile of v6, /device:TPU:2, one launch (start us, length us, event | category | flops | bytes accessed | tf_op | source)
XLA Modules:
  0.0 108.5 jit_solution(5046594412025510233)
XLA Ops:
  0.6 104.3 %shard_map.84 = (bf16[4,32,16,384]{3,2,1,0:T(8,128)(2,1)}, bf16[2,4,8,48,128]{4,3,2,1,0:T(8,128)(2,1)}) custom-call(bf16[32,16,768]{2,1,0:T(8,128)(2,1)} %feat_hbm.3, bf16[32,16,768]{2,1,0:T(8,128)(2,1)} %cot_hbm.3, bf16[2,8,96,96]{3,2,1,0:T(8,128)(2,1)} %wf.1, bf16[2,8,96,96]{3,2,1,0:T(8,128)(2,1)} %ws.1, bf16[5,512,512]{2,1,0:T(8,128)(2,1)} %constant.2.clone.h_tables), custom_call_target="tpu_custom_call" | custom-call | tf_op jit(solution)/shard_map/pallas_call | solution.py:545
  104.9 3.6 %shard_map.85 = (bf16[32,16,768]{2,1,0:T(8,128)(2,1)}, bf16[32,16,768]{2,1,0:T(8,128)(2,1)}, f32[2,8,96,96]{3,2,1,0:T(8,128)}, f32[2,8,96,96]{3,2,1,0:T(8,128)}) custom-call(bf16[32,16,768]{2,1,0:T(8,128)(2,1)} %feat_hbm.3, bf16[32,16,768]{2,1,0:T(8,128)(2,1)} %cot_hbm.3, bf16[4,32,16,384]{3,2,1,0:T(8,128)(2,1)} %get-tuple-element.6.rows_hbm, ...), custom_call_target="tpu_custom_call" | custom-call | tf_op jit(solution)/shard_map/pallas_call | solution.py:595
